TPU v7x, 128 devices: a whole 4x4x4 slice. The times are simulated.
128 devices in a mesh: stretch: 16 (over x, y), head: 8 (over z, core).
Axes of the slice: x: 4, y: 4, z: 4, core: 2. Of those that a mesh axis runs over, the one named last changes fastest.
Arguments:
- q_items: bfloat16 [16, 432, 32, 128], P('stretch', None, 'head'), may hold values from -6 to 6
- k_items: bfloat16 [16, 432, 8, 128], P('stretch', None, 'head'), may hold values from -6 to 6
- v_items: bfloat16 [16, 432, 8, 128], P('stretch', None, 'head'), may hold values from -6 to 6
- d_out: bfloat16 [16, 432, 32, 128], P('stretch', None, 'head'), may hold values from -6 to 6
- reader_query: float32 [2048, 32, 128], P('stretch', 'head'), may hold values from -6 to 6
- reader_span: int32 [2048], P('stretch'), may hold values from 1 to 16
- target: float32 [2048, 4096], P('stretch', 'head'), may hold values from -6 to 6
- out_proj: float32 [4096, 4096], P('stretch', 'head'), may hold values from -0.09375 to 0.09375
Outputs:
- q_items_grad: float32 [16, 432, 32, 128], P('stretch', None, 'head')
- k_items_grad: float32 [16, 432, 8, 128], P('stretch', None, 'head')
- v_items_grad: float32 [16, 432, 8, 128], P('stretch', None, 'head')
- reader_query_grad: float32 [2048, 32, 128], P('stretch', 'head')
- out_proj_grad: float32 [4096, 4096], P('stretch', 'head')
All inputs are finite; a program needn't handle non-finite values.
Results may differ from a plain program's by a relative error of at most 0.0093.
Values may be sent and summed in bfloat16 or wider, within the bound.
No kernel may reach another device: no remote copies, remote signals or barrier semaphores. Data moves between devices by JAX's collectives and lax.ppermute only.
A program may use at most 128 MiB of HBM per device.

v0:
```python
import jax
import jax.numpy as jnp
from jax import lax
from jax.sharding import PartitionSpec as P

SEG_LEN = 384
BEACONS = 48


def sent_together(arrays, axis, dim, along):
    ends, at = ([], 0)
    for a in arrays[:-1]:
        at += a.shape[along]
        ends.append(at)
    both = jnp.concatenate(arrays, axis=along)
    return tuple(jnp.split(lax.all_gather(both, axis, axis=dim, tiled=True), ends, axis=along))


def in_blocks(value, dim, size):
    before, after = (value.shape[:dim], value.shape[dim + 1 :])
    return jnp.moveaxis(value.reshape(*before, size, -1, *after), dim, 0)


def sent_and_summed(value, axis, dim):
    pieces = in_blocks(value, dim, lax.axis_size(axis))
    arrived = lax.all_to_all(pieces, axis, split_axis=0, concat_axis=0, tiled=True)
    return arrived.astype(jnp.float32).sum(axis=0)


def copy_for_each(value, axis):
    size = lax.axis_size(axis)
    return lax.all_to_all(
        jnp.broadcast_to(value[None], (size, *value.shape)), axis, 0, 0, tiled=True
    )


def laid_out(pieces, dim):
    shape = list(pieces.shape[1:])
    shape[dim] *= pieces.shape[0]
    return jnp.moveaxis(pieces, 0, dim).reshape(shape)


def collect(value, axis, dim):
    pieces = copy_for_each(value, axis)
    return laid_out(pieces, dim)


def in_one_piece(arrays, axis, dim, along):
    ends, at = ([], 0)
    for a in arrays[:-1]:
        at += a.shape[along]
        ends.append(at)
    both = jnp.concatenate(arrays, axis=along)
    return tuple(
        jnp.split(lax.psum_scatter(both, axis, scatter_dimension=dim, tiled=True), ends, axis=along)
    )


def narrow_product(pattern, former, latter):
    return jnp.einsum(pattern, former, latter, preferred_element_type=jnp.float32)


def exact_product(pattern, former, latter):
    return jnp.einsum(pattern, former, latter, precision=lax.Precision.HIGHEST)


def softmax_rows(scores, visible):
    masked = jnp.where(visible, scores, -1e30)
    row_top = jnp.max(masked, axis=-1, keepdims=True)
    raised = jnp.where(visible, jnp.exp(masked - row_top), 0.0)
    return raised / jnp.sum(raised, axis=-1, keepdims=True)


def segment_grads(block_index, q_block, k_block, v_block, d_block, beacon_k, beacon_v, key_block):
    item_count, query_heads, head_width = q_block.shape
    groups = k_block.shape[1]
    per_group = query_heads // groups
    scaling = head_width ** (-0.5)
    beacon_count = beacon_k.shape[0]
    all_keys = jnp.concatenate([beacon_k, k_block], axis=0)
    all_values = jnp.concatenate([beacon_v, v_block], axis=0)
    queries = q_block.reshape(item_count, groups, per_group, head_width)
    out_grads = d_block.reshape(item_count, groups, per_group, head_width)
    causal = jnp.arange(item_count)[:, None] >= jnp.arange(item_count)[None, :]
    earlier = jnp.broadcast_to((key_block < block_index)[None, :], (item_count, beacon_count))
    visible = jnp.concatenate([earlier, causal], axis=1)
    scores = narrow_product("sgah,kgh->gask", queries, all_keys) * scaling
    probs = softmax_rows(scores, visible)
    prob_grad = narrow_product("sgah,kgh->gask", out_grads, all_values)
    row_total = jnp.sum(probs * prob_grad, axis=-1, keepdims=True)
    score_grad = (probs * (prob_grad - row_total) * scaling).astype(jnp.bfloat16)
    rounded = probs.astype(jnp.bfloat16)
    q_grad = narrow_product("gask,kgh->sgah", score_grad, all_keys).reshape(
        item_count, query_heads, head_width
    )
    k_grad = narrow_product("gask,sgah->kgh", score_grad, queries)
    v_grad = narrow_product("gask,sgah->kgh", rounded, out_grads)
    return (
        q_grad,
        k_grad[beacon_count:],
        v_grad[beacon_count:],
        k_grad[:beacon_count],
        v_grad[:beacon_count],
    )


def body(q_items, k_items, v_items, d_out, reader_query, reader_span, target, out_proj):
    held_blocks = q_items.shape[0]
    query_heads = q_items.shape[2]
    head_width = q_items.shape[3]
    groups = k_items.shape[2]
    per_group = query_heads // groups
    scaling = head_width ** (-0.5)
    device = lax.axis_index("stretch")
    beacon_k, beacon_v = sent_together(
        (k_items[:, SEG_LEN:], v_items[:, SEG_LEN:]), "stretch", 0, 1
    )
    segments = beacon_k.shape[0]
    beacon_total = segments * BEACONS
    flat_k = beacon_k.reshape(beacon_total, groups, head_width)
    flat_v = beacon_v.reshape(beacon_total, groups, head_width)
    key_block = jnp.arange(beacon_total) // BEACONS
    q_list, k_list, v_list = ([], [], [])
    block_index = device * held_blocks + 0
    q_grad, k_own, v_own, k_far, v_far = segment_grads(
        block_index, q_items[0], k_items[0], v_items[0], d_out[0], flat_k, flat_v, key_block
    )
    q_list.append(q_grad)
    k_list.append(k_own)
    v_list.append(v_own)
    q_items_grad = jnp.stack(q_list)
    k_grads = jnp.stack(k_list)
    v_grads = jnp.stack(v_list)
    readers = reader_query.shape[0]
    wide_k = flat_k.astype(jnp.float32)
    wide_v = flat_v.astype(jnp.float32)
    queries = reader_query.reshape(readers, groups, per_group, head_width)
    visible = key_block[None, :] < reader_span[:, None]
    scores = exact_product("rgah,kgh->gark", queries, wide_k) * scaling
    probs = softmax_rows(scores, visible)
    attended = exact_product("gark,kgh->rgah", probs, wide_v).reshape(
        readers, query_heads * head_width
    )
    along_last = (((1,), (1,)), ((), ()))
    along_first = (((0,), (0,)), ((), ()))
    rows_all = lax.all_gather(out_proj, "stretch", axis=0, tiled=True)
    predicted = lax.dot_general(attended, rows_all, along_last, precision=lax.Precision.HIGHEST)
    columns = sent_and_summed(predicted.astype(jnp.bfloat16), "head", 1)
    errors = collect(columns - target, "head", 1)
    out_proj_grad = sent_and_summed(
        lax.dot_general(errors, attended, along_first, precision=lax.Precision.HIGHEST).astype(
            jnp.bfloat16
        ),
        "stretch",
        0,
    )
    att_grad = jnp.dot(errors, rows_all, precision=lax.Precision.HIGHEST)
    att_grad = att_grad.reshape(readers, groups, per_group, head_width)
    prob_grad = exact_product("rgah,kgh->gark", att_grad, wide_v)
    row_total = jnp.sum(probs * prob_grad, axis=-1, keepdims=True)
    score_grad = probs * (prob_grad - row_total) * scaling
    reader_query_grad = exact_product("gark,kgh->rgah", score_grad, wide_k).reshape(
        readers, query_heads, head_width
    )
    reader_dk = exact_product("gark,rgah->kgh", score_grad, queries)
    reader_dv = exact_product("gark,rgah->kgh", probs, att_grad)
    block_shape = (segments, BEACONS, groups, head_width)
    owned_dk, owned_dv = in_one_piece(
        ((k_far + reader_dk).reshape(block_shape), (v_far + reader_dv).reshape(block_shape)),
        "stretch",
        0,
        1,
    )
    k_items_grad = k_grads.at[:, SEG_LEN:].add(owned_dk)
    v_items_grad = v_grads.at[:, SEG_LEN:].add(owned_dv)
    return (q_items_grad, k_items_grad, v_items_grad, reader_query_grad, out_proj_grad)


def solution(mesh):
    return jax.shard_map(
        body,
        mesh=mesh,
        in_specs=(
            P("stretch", None, "head", None),
            P("stretch", None, "head", None),
            P("stretch", None, "head", None),
            P("stretch", None, "head", None),
            P("stretch", "head", None),
            P("stretch"),
            P("stretch", "head"),
            P("stretch", "head"),
        ),
        out_specs=(
            P("stretch", None, "head", None),
            P("stretch", None, "head", None),
            P("stretch", None, "head", None),
            P("stretch", "head", None),
            P("stretch", "head"),
        ),
        check_vma=False,
    )
```

profile of v0, /device:TPU:0, one launch (start us, length us, event | category | flops | bytes accessed | tf_op | source)
XLA Modules:
  0.0 312.2 jit_solution(9369338249174346727)
XLA Ops:
  7.2 0.0 copy-start
  7.2 0.0 copy-start.9
  7.2 0.0 all-gather.2.cloned.1.call-start
  7.2 0.7 all-gather.2.cloned.1.call-update
  7.9 0.7 slice.79
  8.6 0.7 slice.78
  9.4 24.8 %all_gather.6 = bf16[16,96,1,128]{3,1,2,0:T(8,128)(2,1)S(1)} all-gather(bf16[1,96,1,128]{3,1,2,0:T(8,128)(2,1)S(1)} %pad_maximum_fusion.1), channel_id=1, replica_groups=mesh['stretch'=16,'head'=8] {'stretch'}, dimensions={0}, use_global_device_ids=true | all-gather | bytes 417792 | tf_op jit(solution)/shard_map/all_gather | solution.py:16
  34.2 0.0 copy-start.13
  34.3 0.1 iota_compare_fusion
  34.3 0.8 broadcast_compare_fusion
  35.2 0.0 copy-start.6
  35.2 0.9 fusion.72
  36.1 0.3 fusion.27
  36.4 0.0 copy-start.15
  36.4 0.0 copy-start.26
  36.5 1.0 fusion.24
  37.5 0.2 pad_add_fusion
  37.7 0.0 copy-done.26
  37.8 2.0 fusion.4
  39.8 3.4 %copy-done.2 = f32[1200,432,4]{0,1,2:T(8,128)} copy-done((f32[1200,432,4]{0,1,2:T(8,128)}, f32[1200,432,4]{0,1,2:T(8,128)S(1)}, u32[]{:S(2)}) %copy-start.2) | copy-done | bytes 8294424
  43.2 3.1 fusion.6
  46.3 37.8 %all-gather.2.cloned.1.call-done = f32[4096,512]{1,0:T(8,128)} async-done(((f32[256,512]{1,0:T(8,128)}), f32[4096,512]{1,0:T(8,128)}) %all-gather.2.cloned.1.call-update) | async-done | bytes 8388624 | tf_op jit(solution)/shard_map/all_gather | solution.py:146
  84.1 11.5 %convolution_convert_fusion.1 = bf16[128,4096]{1,0:T(8,128)(2,1)S(1)} fusion(f32[128,512]{0,1:T(8,128)S(1)} %bitcast.224, f32[4096,512]{1,0:T(8,128)} %all-gather.2.cloned.1.call-done), kind=kOutput, calls=%fused_computation.13 | convolution fusion | flops 3221749760 | bytes 9699328 | tf_op jit(solution)/shard_map/dot_general | solution.py:147
  95.7 0.0 copy-start.25
  95.7 1.0 copy.110
  96.7 4.4 %all-to-all-start = ((bf16[8,128,512]{2,1,0:T(8,128)(2,1)}), bf16[8,128,512]{2,1,0:T(8,128)(2,1)S(1)}, u32[]{:S(2)}, u32[]{:S(2)}) async-start(bf16[8,128,512]{2,1,0:T(8,128)(2,1)} %bitcast.209), calls=%async_computation | async-start | bytes 2097152 | tf_op jit(solution)/shard_map/all_to_all | solution.py:26
  101.2 0.0 copy-start.8
  101.2 8.7 %fusion = (f32[4,432]{1,0:T(4,128)}, f32[1200,432,4]{0,1,2:T(8,128)}) fusion(f32[4,432]{1,0:T(4,128)S(1)} %fusion.6, f32[4,432]{1,0:T(4,128)S(1)} %get-tuple-element.46, f32[1200,432,4]{0,1,2:T(8,128)} %copy-done.2, pred[432,1200]{1,0:T(8,128)(4,1)S(1)} %pad_add_fusion, bf16[432,4,128]{2,1,0:T(4,128)(2,1)S(1)} %bitcast.210, ...), kind=kOutput, calls=%fused_computation.3 | convolution fusion | flops 545969472 | bytes 17877504 | tf_op jit(solution)/shard_map/sgah,kgh->gask/dot_general | solution.py:60
  109.9 7.2 %all-to-all-done = bf16[8,128,512]{2,1,0:T(8,128)(2,1)S(1)} async-done(((bf16[8,128,512]{2,1,0:T(8,128)(2,1)}), bf16[8,128,512]{2,1,0:T(8,128)(2,1)S(1)}, u32[]{:S(2)}, u32[]{:S(2)}) %all-to-all-start) | async-done | bytes 1048608 | tf_op jit(solution)/shard_map/all_to_all | solution.py:26
  117.1 0.1 convert_reduce_fusion.1
  117.3 1.6 broadcast_in_dim.53
  118.9 3.6 %all-to-all-start.1 = ((f32[8,128,512]{2,1,0:T(8,128)}), f32[8,128,512]{2,1,0:T(8,128)S(1)}, u32[]{:S(2)}, u32[]{:S(2)}) async-start(f32[8,128,512]{2,1,0:T(8,128)} %broadcast_in_dim.53), calls=%async_computation.1 | async-start | bytes 4194304 | tf_op jit(solution)/shard_map/all_to_all | solution.py:32
  122.5 10.3 %fusion.7 = bf16[4,432,1200]{2,1,0:T(8,128)(2,1)} fusion(f32[1200,432,4]{0,1,2:T(8,128)} %get-tuple-element.49, f32[4,432]{1,0:T(4,128)} %get-tuple-element.48, f32[4,432]{1,0:T(4,128)} %copy-done.21, f32[4,432]{1,0:T(4,128)} %copy-done.19, f32[1200,432,4]{0,1,2:T(8,128)} %copy-done.2, pred[432,1200]{1,0:T(8,128)(4,1)S(1)} %pad_add_fusion), kind=kLoop, calls=%fused_computation.14 | loop fusion | flops 18662400 | bytes 21275136 | tf_op jit(solution)/shard_map/reshape.88
  132.8 16.9 %all-to-all-done.1 = f32[8,128,512]{2,1,0:T(8,128)S(1)} async-done(((f32[8,128,512]{2,1,0:T(8,128)}), f32[8,128,512]{2,1,0:T(8,128)S(1)}, u32[]{:S(2)}, u32[]{:S(2)}) %all-to-all-start.1) | async-done | bytes 2097184 | tf_op jit(solution)/shard_map/all_to_all | solution.py:32
  149.6 0.2 copy.90
  149.8 8.4 %convolution_convert_fusion = bf16[4096,512]{1,0:T(8,128)(2,1)} fusion(f32[128,4096]{1,0:T(8,128)S(1)} %bitcast.217, f32[128,512]{0,1:T(8,128)S(1)} %bitcast.225), kind=kOutput, calls=%fused_computation.12 | convolution fusion | flops 3223322624 | bytes 6553600 | tf_op jit(solution)/shard_map/dot_general | solution.py:151
  158.3 5.4 %all-to-all-start.2 = ((bf16[16,256,512]{2,1,0:T(8,128)(2,1)}), bf16[16,256,512]{2,1,0:T(8,128)(2,1)}, u32[]{:S(2)}, u32[]{:S(2)}) async-start(bf16[16,256,512]{2,1,0:T(8,128)(2,1)} %bitcast.214), calls=%async_computation.2 | async-start | bytes 8388608 | tf_op jit(solution)/shard_map/all_to_all | solution.py:26
  163.7 0.3 all-reduce.3.cloned.1.call-start
  164.0 0.0 copy-start.27
  164.0 7.0 %fusion.12 = f32[1200,1,128]{2,0,1:T(8,128)} fusion(f32[4,432]{1,0:T(4,128)S(1)} %copy-done.22, f32[4,432]{1,0:T(4,128)S(1)} %copy-done.20, f32[1200,432,4]{0,1,2:T(8,128)} %copy-done.2, pred[432,1200]{1,0:T(8,128)(4,1)S(1)} %pad_add_fusion, bf16[432,4,128]{2,1,0:T(4,128)(2,1)S(1)} %bitcast.211), kind=kOutput, calls=%fused_computation.18 | convolution fusion | flops 543283200 | bytes 9883392 | tf_op jit(solution)/shard_map/gask,sgah->kgh/dot_general | solution.py:60
  171.1 4.5 %convolution_bitcast_fusion = f32[1200,1,128]{2,0,1:T(8,128)} fusion(bf16[4,432,1200]{2,1,0:T(8,128)(2,1)} %fusion.7, bf16[432,4,128]{2,1,0:T(4,128)(2,1)S(1)} %bitcast.237), kind=kOutput, calls=%fused_computation.19 | convolution fusion | flops 530841600 | bytes 5203968 | tf_op jit(solution)/shard_map/gask,sgah->kgh/dot_general | solution.py:60
  175.6 8.9 %copy.65 = f32[512,4096]{1,0:T(8,128)} copy(f32[512,4096]{0,1:T(8,128)} %bitcast.212) | data formatting | bytes 16777216 | tf_op jit(solution)/shard_map/dot_general | solution.py:157
  184.5 2.5 copy.64
  187.1 1.7 reshape.278
  188.8 0.0 copy-start.7
  188.9 11.3 %fusion.73 = f32[128,4,128]{2,0,1:T(8,128)S(1)} fusion(f32[128,4096,1]{1,0,2:T(8,128)S(1)} %reshape.278, f32[4,128,4096]{2,1,0:T(8,128)} %bitcast.213), kind=kOutput, calls=%fused_computation.87 | convolution fusion | flops 3221225472 | bytes 10747904 | tf_op jit(solution)/shard_map/dot_general | solution.py:157
  200.2 1.4 fusion.37
  201.7 1.1 fusion.19
  202.8 0.0 copy-done.18
  202.8 1.8 fusion.34
  204.6 0.0 copy-start.16
  204.6 1.0 pad_maximum_fusion
  205.6 0.0 all-reduce.3.cloned.1.call-update
  205.7 0.0 copy-start.28
  205.7 3.6 %convolution_bitcast_fusion.1 = f32[1,432,4,128]{3,1,2,0:T(8,128)S(1)} fusion(bf16[4,432,1200]{2,1,0:T(8,128)(2,1)} %fusion.7, bf16[432,1,128]{2,0,1:T(8,128)(2,1)S(1)} %bitcast.234, bf16[768,1,128]{2,0,1:T(8,128)(2,1)S(1)} %bitcast.221), kind=kOutput, calls=%fused_computation.37 | convolution fusion | flops 531456000 | bytes 5339136 | tf_op jit(solution)/shard_map/gask,kgh->sgah/dot_general | solution.py:60
  209.3 1.3 copy.75
  210.5 0.6 dynamic-slice.18
  211.1 1.1 slice_bitcast_fusion
  212.2 2.6 fusion.40
  214.8 0.8 copy.78
  215.6 84.5 %all-reduce.3.cloned.1.call-done = f32[16,96,1,128]{3,1,2,0:T(8,128)} async-done(((f32[16,96,1,128]{3,1,2,0:T(8,128)}), f32[16,96,1,128]{3,1,2,0:T(8,128)}) %all-reduce.3.cloned.1.call-update) | async-done | bytes 786448
  300.1 1.5 fusion.55
  301.6 0.0 copy-start.11
  301.6 3.7 %convert_reduce_fusion = f32[256,512]{1,0:T(8,128)} fusion(bf16[16,256,512]{2,1,0:T(8,128)(2,1)} %all-to-all-done.2), kind=kLoop, calls=%fused_computation.8 | loop fusion | flops 4063232 | bytes 4718592 | tf_op jit(solution)/shard_map/reduce_sum | solution.py:27
  (52 shorter events, 0.2 us)
Async XLA Ops:
  7.2 94.0 %copy-start = (bf16[1,432,4,128]{3,2,1,0:T(4,128)(2,1)S(1)}, bf16[1,432,4,128]{3,2,1,0:T(4,128)(2,1)}, u32[]{:S(2)}) copy-start(bf16[1,432,4,128]{3,2,1,0:T(4,128)(2,1)} %param.15) | copy-start | bytes 1327108
  7.2 28.0 %copy-start.9 = (f32[128,4,128]{2,1,0:T(4,128)S(1)}, f32[128,4,128]{2,1,0:T(4,128)}, u32[]{:S(2)}) copy-start(f32[128,4,128]{2,1,0:T(4,128)} %param.16) | copy-start | bytes 786436
  7.2 77.0 %all-gather.2.cloned.1.call-start = ((), (), s32[]{:S(2)}) async-start(), calls=%async_computation.3 | async-start | bytes 8912896 | tf_op jit(solution)/shard_map/all_gather | solution.py:146
  34.2 66.9 %copy-start.13 = (bf16[16,48,1,128]{3,1,0,2:T(8,128)(2,1)}, bf16[16,48,1,128]{3,1,0,2:T(8,128)(2,1)S(1)}, u32[]{:S(2)}) copy-start(bf16[16,48,1,128]{3,1,0,2:T(8,128)(2,1)S(1)} %split.17) | copy-start | bytes 589828
  35.2 2.3 copy-start.6
  36.1 1.4 copy-start.3
  36.4 1.1 copy-start.23
  36.4 1.3 copy-start.15
  36.4 1.3 copy-start.26
  39.8 3.4 %copy-start.2 = (f32[1200,432,4]{0,1,2:T(8,128)}, f32[1200,432,4]{0,1,2:T(8,128)S(1)}, u32[]{:S(2)}) copy-start(f32[1200,432,4]{0,1,2:T(8,128)S(1)} %get-tuple-element.47) | copy-start | bytes 24883204
  39.8 61.4 %copy-start.19 = (f32[4,432]{1,0:T(4,128)}, f32[4,432]{1,0:T(4,128)S(1)}, u32[]{:S(2)}) copy-start(f32[4,432]{1,0:T(4,128)S(1)} %get-tuple-element.46) | copy-start | bytes 20740
  46.3 54.9 %copy-start.21 = (f32[4,432]{1,0:T(4,128)}, f32[4,432]{1,0:T(4,128)S(1)}, u32[]{:S(2)}) copy-start(f32[4,432]{1,0:T(4,128)S(1)} %fusion.6) | copy-start | bytes 20740
  95.7 5.5 %copy-start.25 = (bf16[1,432,1,128]{3,1,2,0:T(8,128)(2,1)S(1)}, bf16[1,432,1,128]{3,1,2,0:T(8,128)(2,1)}, u32[]{:S(2)}) copy-start(bf16[1,432,1,128]{3,1,2,0:T(8,128)(2,1)} %param.14) | copy-start | bytes 331780
  96.7 20.4 %all-to-all-start = ((bf16[8,128,512]{2,1,0:T(8,128)(2,1)}), bf16[8,128,512]{2,1,0:T(8,128)(2,1)S(1)}, u32[]{:S(2)}, u32[]{:S(2)}) async-start(bf16[8,128,512]{2,1,0:T(8,128)(2,1)} %bitcast.209), calls=%async_computation | async-start | bytes 2097152 | tf_op jit(solution)/shard_map/all_to_all | solution.py:26
  101.2 16.1 %copy-start.8 = (f32[128,512]{1,0:T(8,128)S(1)}, f32[128,512]{1,0:T(8,128)}, u32[]{:S(2)}) copy-start(f32[128,512]{1,0:T(8,128)} %param.18) | copy-start | bytes 786436
  118.9 30.7 %all-to-all-start.1 = ((f32[8,128,512]{2,1,0:T(8,128)}), f32[8,128,512]{2,1,0:T(8,128)S(1)}, u32[]{:S(2)}, u32[]{:S(2)}) async-start(f32[8,128,512]{2,1,0:T(8,128)} %broadcast_in_dim.53), calls=%async_computation.1 | async-start | bytes 4194304 | tf_op jit(solution)/shard_map/all_to_all | solution.py:32
  158.3 5.7 %copy-start.20 = (f32[4,432]{1,0:T(4,128)S(1)}, f32[4,432]{1,0:T(4,128)}, u32[]{:S(2)}) copy-start(f32[4,432]{1,0:T(4,128)} %copy-done.19) | copy-start | bytes 20740
  158.3 5.7 %copy-start.22 = (f32[4,432]{1,0:T(4,128)S(1)}, f32[4,432]{1,0:T(4,128)}, u32[]{:S(2)}) copy-start(f32[4,432]{1,0:T(4,128)} %copy-done.21) | copy-start | bytes 20740
  158.3 143.4 %all-to-all-start.2 = ((bf16[16,256,512]{2,1,0:T(8,128)(2,1)}), bf16[16,256,512]{2,1,0:T(8,128)(2,1)}, u32[]{:S(2)}, u32[]{:S(2)}) async-start(bf16[16,256,512]{2,1,0:T(8,128)(2,1)} %bitcast.214), calls=%async_computation.2 | async-start | bytes 8388608 | tf_op jit(solution)/shard_map/all_to_all | solution.py:26
  163.7 136.4 %all-reduce.3.cloned.1.call-start = ((), (), s32[]{:S(2)}) async-start(), calls=%async_computation.4 | async-start | bytes 1572864
  164.0 7.1 %copy-start.27 = (bf16[1,432,4,128]{3,2,1,0:T(4,128)(2,1)S(1)}, bf16[1,432,4,128]{3,2,1,0:T(4,128)(2,1)}, u32[]{:S(2)}) copy-start(bf16[1,432,4,128]{3,2,1,0:T(4,128)(2,1)} %param.12) | copy-start | bytes 1327108
  188.8 11.3 %copy-start.4 = (f32[1,4,128,768]{2,3,1,0:T(8,128)S(1)}, f32[1,4,128,768]{2,3,1,0:T(8,128)}, u32[]{:S(2)}) copy-start(f32[1,4,128,768]{2,3,1,0:T(8,128)} %copy-done.3) | copy-start | bytes 4718596
  188.8 11.3 %copy-start.7 = (pred[128,768]{0,1:T(8,128)(4,1)S(1)}, pred[128,768]{0,1:T(8,128)(4,1)}, u32[]{:S(2)}) copy-start(pred[128,768]{0,1:T(8,128)(4,1)} %copy-done.6) | copy-start | bytes 294916
  188.8 11.3 %copy-start.17 = (f32[1200,1,128]{2,0,1:T(8,128)S(1)}, f32[1200,1,128]{2,0,1:T(8,128)}, u32[]{:S(2)}) copy-start(f32[1200,1,128]{2,0,1:T(8,128)} %fusion.12) | copy-start | bytes 1843204
  188.9 11.3 %copy-start.24 = (f32[4,128]{1,0:T(4,128)S(1)}, f32[4,128]{1,0:T(4,128)}, u32[]{:S(2)}) copy-start(f32[4,128]{1,0:T(4,128)} %copy-done.23) | copy-start | bytes 6148
  200.2 1.5 copy-start.14
  201.6 1.1 copy-start.10
  201.7 1.1 copy-start.18
  202.7 1.9 copy-start.29
  204.6 1.0 copy-start.16
  205.7 4.9 %copy-start.28 = (u32[128]{0:T(128)S(1)}, u32[128]{0:T(128)}, u32[]{:S(2)}) copy-start(u32[128]{0:T(128)} %constant.81) | copy-start | bytes 1540
  209.2 2.9 copy-start.5
  300.1 5.3 %copy-start.1 = (bf16[1,432,4,128]{3,2,1,0:T(4,128)(2,1)S(1)}, bf16[1,432,4,128]{3,2,1,0:T(4,128)(2,1)}, u32[]{:S(2)}) copy-start(bf16[1,432,4,128]{3,2,1,0:T(4,128)(2,1)} %param.15) | copy-start | bytes 1327108
  301.6 3.8 %copy-start.11 = (f32[1,432,1,128]{3,1,2,0:T(8,128)}, f32[1,432,1,128]{3,1,2,0:T(8,128)S(1)}, u32[]{:S(2)}) copy-start(f32[1,432,1,128]{3,1,2,0:T(8,128)S(1)} %get-tuple-element.44) | copy-start | bytes 663556
  301.6 3.8 %copy-start.12 = (f32[1,432,1,128]{3,1,2,0:T(8,128)}, f32[1,432,1,128]{3,1,2,0:T(8,128)S(1)}, u32[]{:S(2)}) copy-start(f32[1,432,1,128]{3,1,2,0:T(8,128)S(1)} %get-tuple-element.45) | copy-start | bytes 663556
Sparse Core Ops, SparseCore 0:
  10.2 73.9 all-gather.1
  205.8 94.2 all-reduce.2
where the time goes:
time: 313 us; the launch traced here: 312 us
  waiting for transfers between devices  147 us (47%)
  matrix products  65.9 us (21%)
  local copies, waits for them, and re-layouts  24.9 us (8%)
  blocking collectives  24.8 us (8%)
  other arithmetic  21.2 us (7%)
  between operations  14.6 us (5%)
  starting transfers between devices  13.8 us (4%)
    unnamed x3, waiting for transfers between devices  85.2 us
    all_gather x1, waiting for transfers between devices, body(): rows_all = lax.all_gather(out_proj, 'stretch', axis=0, tiled=True)  37.8 us
    dot_general x5, matrix products, narrow_product(): jnp.einsum(pattern, former, latter, preferred_element_type=jnp.float32)  25.8 us
    all_gather x1, blocking collectives, sent_together(): lax.all_gather(both, axis, axis=dim, tiled=True)  24.8 us
    all_to_all x1, waiting for transfers between devices, copy_for_each(): lax.all_to_all(jnp.broadcast_to(value[None], (size, *value.shape)), axis,...  16.9 us
    dot_general x1, matrix products, body(): lax.dot_general(attended, rows_all, along_last, precision=lax.Precision.H...  11.5 us
    dot_general x1, matrix products, body(): att_grad = jnp.dot(errors, rows_all, precision=lax.Precision.HIGHEST)  11.3 us
    another operation x1, other arithmetic  10.3 us
  transfers between devices with their start and end apart: 5, of which 4 were waited for; matrix products, arithmetic and copies ran while one was open for 26% of the time, Pallas kernels for 0%

commit v1 on v0

v1 whole, which is shorter than its diff:
```python
import jax
import jax.numpy as jnp
from jax import lax
from jax.experimental import pallas as pl
from jax.experimental.pallas import tpu as pltpu
from jax.sharding import Mesh
from jax.sharding import PartitionSpec as P

SEG_LEN = 384
BEACONS = 48
ITEMS = SEG_LEN + BEACONS
SEGMENTS = 16
HEADS = 4
WIDTH = 128
KEYS = SEGMENTS * BEACONS
READERS = 128
FEATURES = HEADS * WIDTH
SIDE = 4
ROWS = SIDE * READERS
TILE = 896
PADDED = 2 * TILE
CHUNK = 192
SCALING = WIDTH ** (-0.5)
HIDDEN = -1e30
LIMIT = 48 * 1024 * 1024
STRETCH = ("x", "y")
HEAD = ("z", "core")

bf16 = jnp.bfloat16
f32 = jnp.float32


def nn(a, b):
    return lax.dot_general(a, b, (((1,), (0,)), ((), ())), preferred_element_type=f32)


def nt(a, b):
    return lax.dot_general(a, b, (((1,), (1,)), ((), ())), preferred_element_type=f32)


def tn(a, b):
    return lax.dot_general(a, b, (((0,), (0,)), ((), ())), preferred_element_type=f32)


def halves(value):
    high = value.astype(bf16)
    return high, (value - high.astype(f32)).astype(bf16)


def shifted(value, axis, by):
    size = lax.axis_size(axis)
    return lax.ppermute(value, axis, [(i, (i + by) % size) for i in range(size)])


def whole(shape, dtype):
    return jax.ShapeDtypeStruct(shape, dtype)


def kernel_call(kernel, outs, scratch=(), flops=0, moved=0, scalars=True, inputs=1):
    vmem = pl.BlockSpec(memory_space=pltpu.VMEM)
    first = [pl.BlockSpec(memory_space=pltpu.SMEM)] if scalars else []
    return pl.pallas_call(
        kernel,
        out_shape=outs,
        in_specs=first + [vmem] * inputs,
        out_specs=jax.tree.map(lambda _: vmem, outs),
        scratch_shapes=list(scratch),
        compiler_params=pltpu.CompilerParams(vmem_limit_bytes=LIMIT),
        cost_estimate=pl.CostEstimate(flops=flops, transcendentals=0, bytes_accessed=moved),
    )


def segment_kernel(place, q, d, far_kv, own_kv, dq, far, own, score, grad):
    seen_beacons = place[0] * BEACONS

    for t in range(2):
        rows = pl.ds(t * TILE, TILE)
        own_chunks = [(0, 224)] if t == 0 else [(0, 224), (224, 208)]
        q_t = q[rows, :]
        d_t = d[rows, :]

        def far_scores(i, top):
            at = pl.multiple_of(i * CHUNK, CHUNK)
            s = nt(far_kv[pl.ds(at, CHUNK), :WIDTH], q_t) * SCALING
            key = lax.broadcasted_iota(jnp.int32, s.shape, 0) + at
            s = jnp.where(key < seen_beacons, s, HIDDEN)
            score[pl.ds(at, CHUNK), :] = s
            return jnp.maximum(top, jnp.max(s, axis=0, keepdims=True))

        top = jnp.full((1, TILE), HIDDEN, f32)
        top = lax.fori_loop(0, KEYS // CHUNK, far_scores, top)
        for at, count in own_chunks:
            s = nt(own_kv[pl.ds(at, count), :WIDTH], q_t) * SCALING
            key = lax.broadcasted_iota(jnp.int32, s.shape, 0) + at
            item = (lax.broadcasted_iota(jnp.int32, s.shape, 1) + t * TILE) >> 2
            s = jnp.where(key <= item, s, HIDDEN)
            score[pl.ds(KEYS + at, count), :] = s
            top = jnp.maximum(top, jnp.max(s, axis=0, keepdims=True))

        def raised(at, count, v, sums):
            e = jnp.exp(score[pl.ds(at, count), :] - top)
            g = nt(v, d_t)
            score[pl.ds(at, count), :] = e
            grad[pl.ds(at, count), :] = g
            return (
                sums[0] + jnp.sum(e, axis=0, keepdims=True),
                sums[1] + jnp.sum(e * g, axis=0, keepdims=True),
            )

        def far_raised(i, sums):
            at = pl.multiple_of(i * CHUNK, CHUNK)
            return raised(at, CHUNK, far_kv[pl.ds(at, CHUNK), WIDTH:], sums)

        sums = (jnp.zeros((1, TILE), f32), jnp.zeros((1, TILE), f32))
        sums = lax.fori_loop(0, KEYS // CHUNK, far_raised, sums)
        for at, count in own_chunks:
            sums = raised(KEYS + at, count, own_kv[pl.ds(at, count), WIDTH:], sums)
        inverse = 1.0 / sums[0]
        total = sums[1] * inverse

        def grads(at, count, k):
            p = score[pl.ds(at, count), :] * inverse
            ds = (p * (grad[pl.ds(at, count), :] - total) * SCALING).astype(bf16)
            return nn(ds, q_t), nn(p.astype(bf16), d_t), tn(k, ds)

        def far_grads(i, acc):
            at = pl.multiple_of(i * CHUNK, CHUNK)
            dk, dv, part = grads(at, CHUNK, far_kv[pl.ds(at, CHUNK), :WIDTH])
            if t == 0:
                far[pl.ds(at, CHUNK), :WIDTH] = dk
                far[pl.ds(at, CHUNK), WIDTH:] = dv
            else:
                far[pl.ds(at, CHUNK), :WIDTH] += dk
                far[pl.ds(at, CHUNK), WIDTH:] += dv
            return acc + part

        acc = lax.fori_loop(0, KEYS // CHUNK, far_grads, jnp.zeros((WIDTH, TILE), f32))
        for at, count in own_chunks:
            dk, dv, part = grads(KEYS + at, count, own_kv[pl.ds(at, count), :WIDTH])
            acc = acc + part
            if t == 1 and at == 0:
                own[pl.ds(at, count), :WIDTH] += dk
                own[pl.ds(at, count), WIDTH:] += dv
            else:
                own[pl.ds(at, count), :WIDTH] = dk
                own[pl.ds(at, count), WIDTH:] = dv
        dq[rows, :] = acc.T


def reader_kernel(seen, q, kv, probs, attended):
    k = kv[:, :WIDTH]
    v = kv[:, WIDTH:]
    for h in range(0, HEADS, 2):
        cols = pl.ds(h * READERS, 2 * READERS)
        q_all = q[cols, :]
        q_0 = q_all.astype(bf16)
        q_1, q_2 = halves(q_all - q_0.astype(f32))
        s = (nt(k, q_0) + nt(k, q_1) + nt(k, q_2)) * SCALING
        key = lax.broadcasted_iota(jnp.int32, s.shape, 0)
        s = jnp.where(key < seen[:, cols], s, HIDDEN)
        e = jnp.exp(s - jnp.max(s, axis=0, keepdims=True))
        p = e * (1.0 / jnp.sum(e, axis=0, keepdims=True))
        probs[:, cols] = p
        high, low = halves(p)
        out = tn(v, high) + tn(v, low)
        for i in range(2):
            at = (h + i) * WIDTH
            attended[:, at : at + WIDTH] = out[:, i * READERS : (i + 1) * READERS].T.astype(bf16)


def reader_grad_kernel(g_0, g_1, g_2, g_3, probs, q, kv, far, dq, beacon_grad):
    k = kv[:, :WIDTH]
    v = kv[:, WIDTH:]
    dk = far[:, :WIDTH]
    dv = far[:, WIDTH:]
    for h in range(0, HEADS, 2):
        cols = pl.ds(h * READERS, 2 * READERS)
        g = []
        for i in range(2):
            at = slice((h + i) * WIDTH, (h + i + 1) * WIDTH)
            g.append(
                g_0[:, at] + g_1[:, at].astype(f32) + g_2[:, at].astype(f32) + g_3[:, at].astype(f32)
            )
        high, low = halves(jnp.concatenate(g, axis=0))
        p = probs[:, cols]
        pg = nt(v, high) + nt(v, low)
        total = jnp.sum(p * pg, axis=0, keepdims=True)
        ds_high, ds_low = halves(p * (pg - total) * SCALING)
        out = tn(k, ds_high) + tn(k, ds_low)
        for i in range(2):
            dq[:, h + i, :] = out[:, i * READERS : (i + 1) * READERS].T
        dk = dk + nn(ds_high, q[cols, :].astype(bf16))
        dv = dv + nn(p.astype(bf16), high)
    beacon_grad[:, :WIDTH] = dk.astype(bf16)
    beacon_grad[:, WIDTH:] = dv.astype(bf16)


def predict_kernel(place, a_0, a_1, a_2, a_3, w, own, other):
    z = place[1]
    core = place[2]
    a = jnp.concatenate([a_0[...], a_1[...], a_2[...], a_3[...]], axis=0)
    for i in range(SIDE):
        at = lax.rem(z + i, SIDE)
        other[i] = nt(a, w[at, 1 - core]).astype(bf16)
        own[i] = nt(a, w[at, core])


def gather_errors(place, mine, others, errors):
    z = place[1]
    core = place[2]
    for i in range(SIDE):
        at = lax.rem(z + SIDE - i, SIDE)
        errors[at, core] = mine[i][...]
        errors[at, 1 - core] = others[i][...]


def attended_grad_kernel(place, e_0, e_1, e_2, e_3, o_0, o_1, o_2, o_3, w, g_0, g_1, g_2, g_3, errors):
    gather_errors(place, (e_0, e_1, e_2, e_3), (o_0, o_1, o_2, o_3), errors)
    for i, out in enumerate((g_0, g_1, g_2, g_3)):
        rows = pl.ds(i * READERS, READERS)
        acc = jnp.zeros((READERS, FEATURES), f32)
        for b in range(SIDE):
            e = jnp.concatenate([errors[b, 0, rows, :], errors[b, 1, rows, :]], axis=1)
            acc = acc + nn(e, jnp.concatenate([w[b, 0], w[b, 1]], axis=0))
        out[...] = acc.astype(out.dtype)


def projection_grad_kernel(
    place, e_0, e_1, e_2, e_3, o_0, o_1, o_2, o_3, a_0, a_1, a_2, a_3, p_0, p_1, p_2, p_3, errors
):
    gather_errors(place, (e_0, e_1, e_2, e_3), (o_0, o_1, o_2, o_3), errors)
    x = place[3]
    a = jnp.concatenate([a_0[...], a_1[...], a_2[...], a_3[...]], axis=0)
    for i, out in enumerate((p_0, p_1, p_2, p_3)):
        at = lax.rem(x + i, SIDE)
        for half in range(2):
            out[half * WIDTH : (half + 1) * WIDTH, :] = tn(errors[at, half], a).astype(bf16)


def body(q_items, k_items, v_items, d_out, reader_query, reader_span, target, out_proj):
    x = lax.axis_index("x")
    y = lax.axis_index("y")
    z = lax.axis_index("z")
    core = lax.axis_index("core")
    place = jnp.stack([x * SIDE + y, z, core, x]).astype(jnp.int32)

    w_all = lax.all_gather(out_proj.astype(bf16), "x", axis=0, tiled=True)
    w_all = w_all.reshape(SIDE, 2, WIDTH, FEATURES)

    own_kv = jnp.concatenate(
        [k_items.reshape(ITEMS, WIDTH), v_items.reshape(ITEMS, WIDTH)], axis=1
    )
    sent = jnp.broadcast_to(own_kv[None, SEG_LEN:], (SEGMENTS, BEACONS, 2 * WIDTH))
    far_kv = lax.all_to_all(sent, STRETCH, 0, 0, tiled=True).reshape(KEYS, 2 * WIDTH)

    parts = target.reshape(READERS, 2, 2, WIDTH).transpose(2, 1, 0, 3)
    kept = lax.dynamic_index_in_dim(parts, core, 0, keepdims=False)
    swapped = lax.ppermute(
        lax.dynamic_index_in_dim(parts, 1 - core, 0, keepdims=False), "core", [(0, 1), (1, 0)]
    )
    by_y = jnp.concatenate(
        [jnp.where(core == 0, kept, swapped), jnp.where(core == 0, swapped, kept)], axis=0
    )
    targets = [
        lax.dynamic_index_in_dim(by_y, lax.rem(y + i, SIDE), 0, keepdims=False) for i in range(SIDE)
    ]
    targets = [targets[0]] + [shifted(targets[i], "y", i) for i in range(1, SIDE)]

    rq = reader_query.transpose(1, 0, 2).reshape(HEADS * READERS, WIDTH)
    seen = jnp.tile(reader_span * BEACONS, HEADS)[None, :]
    probs, attended = kernel_call(
        reader_kernel,
        (whole((KEYS, HEADS * READERS), f32), whole((READERS, FEATURES), bf16)),
        scalars=False,
        inputs=3,
        flops=5 * 2 * KEYS * HEADS * READERS * WIDTH,
        moved=3 * 1024 * 1024,
    )(seen, rq, far_kv)

    a = [attended] + [shifted(attended, "y", i) for i in range(1, SIDE)]

    pad = ((0, PADDED - ITEMS * HEADS), (0, 0))
    q_rows = jnp.pad(q_items.reshape(ITEMS * HEADS, WIDTH), pad)
    d_rows = jnp.pad(d_out.reshape(ITEMS * HEADS, WIDTH), pad)
    dq_rows, far_grad, own_grad = kernel_call(
        segment_kernel,
        (
            whole((PADDED, WIDTH), f32),
            whole((KEYS, 2 * WIDTH), f32),
            whole((ITEMS, 2 * WIDTH), f32),
        ),
        scratch=(
            pltpu.VMEM((KEYS + ITEMS, TILE), f32),
            pltpu.VMEM((KEYS + ITEMS, TILE), f32),
        ),
        inputs=4,
        flops=5 * 2 * (KEYS + ITEMS) * PADDED * WIDTH,
        moved=4 * 1024 * 1024,
    )(place, q_rows, d_rows, far_kv, own_kv)

    own, other = kernel_call(
        predict_kernel,
        (whole((SIDE, ROWS, WIDTH), f32), whole((SIDE, ROWS, WIDTH), bf16)),
        inputs=5,
        flops=2 * ROWS * FEATURES * 1024,
        moved=3 * 1024 * 1024,
    )(place, *a, w_all)
    from_core = lax.ppermute(other, "core", [(0, 1), (1, 0)])
    chip = own + from_core.astype(f32)
    arrived = [shifted(chip[i].astype(bf16), "z", i) for i in range(1, SIDE)]
    total = chip[0] - jnp.concatenate(targets, axis=0)
    for part in arrived:
        total = total + part.astype(f32)
    error = total.astype(bf16)

    mine = [error] + [shifted(error, "z", i) for i in range(1, SIDE)]
    others = [lax.ppermute(e, "core", [(0, 1), (1, 0)]) for e in mine]
    stack = pltpu.VMEM((SIDE, 2, ROWS, WIDTH), bf16)
    piece = (READERS, FEATURES)
    g = kernel_call(
        attended_grad_kernel,
        (whole(piece, f32), whole(piece, bf16), whole(piece, bf16), whole(piece, bf16)),
        scratch=(stack,),
        inputs=9,
        flops=2 * ROWS * FEATURES * 1024,
        moved=3 * 1024 * 1024,
    )(place, *mine, *others, w_all)
    g = [g[0]] + [shifted(g[i], "y", -i) for i in range(1, SIDE)]

    block = whole((2 * WIDTH, FEATURES), bf16)
    w_grad = kernel_call(
        projection_grad_kernel,
        (block,) * SIDE,
        scratch=(stack,),
        inputs=12,
        flops=2 * ROWS * FEATURES * 1024,
        moved=3 * 1024 * 1024,
    )(place, *mine, *others, *a)
    out_proj_grad = w_grad[0].astype(f32)
    for i in range(1, SIDE):
        out_proj_grad = out_proj_grad + shifted(w_grad[i], "x", i).astype(f32)

    reader_query_grad, beacon_grad = kernel_call(
        reader_grad_kernel,
        (whole((READERS, HEADS, WIDTH), f32), whole((KEYS, 2 * WIDTH), bf16)),
        scalars=False,
        inputs=8,
        flops=8 * 2 * KEYS * HEADS * READERS * WIDTH,
        moved=5 * 1024 * 1024,
    )(*g, probs, rq, far_kv, far_grad)

    pieces = beacon_grad.reshape(SEGMENTS, BEACONS, 2 * WIDTH)
    owned = lax.all_to_all(pieces, STRETCH, 0, 0, tiled=True).astype(f32).sum(axis=0)
    own_grad = own_grad.at[SEG_LEN:].add(owned)
    q_items_grad = dq_rows[: ITEMS * HEADS].reshape(1, ITEMS, HEADS, WIDTH)
    k_items_grad = own_grad[:, :WIDTH].reshape(1, ITEMS, 1, WIDTH)
    v_items_grad = own_grad[:, WIDTH:].reshape(1, ITEMS, 1, WIDTH)
    return q_items_grad, k_items_grad, v_items_grad, reader_query_grad, out_proj_grad


def solution(mesh):
    axes = Mesh(mesh.devices.reshape(SIDE, SIDE, SIDE, 2), STRETCH + HEAD)
    items = P(STRETCH, None, HEAD, None)
    return jax.shard_map(
        body,
        mesh=axes,
        in_specs=(
            items,
            items,
            items,
            items,
            P(STRETCH, HEAD, None),
            P(STRETCH),
            P(STRETCH, HEAD),
            P(STRETCH, HEAD),
        ),
        out_specs=(items, items, items, P(STRETCH, HEAD, None), P(STRETCH, HEAD)),
        check_vma=False,
    )
```

time: 313 us -> 126 us (0.40)
  waiting for transfers between devices: 147 us -> 29.5 us
  matrix products: 65.9 us -> 0 us
  starting transfers between devices: 13.8 us -> 40.9 us
  blocking collectives: 24.8 us -> 0 us
  Pallas kernels: 0 us -> 23.8 us
  local copies, waits for them, and re-layouts: 24.9 us -> 9.51 us
  other arithmetic: 21.2 us -> 7.12 us
    unnamed x3 -> x1, waiting for transfers between devices: 85.2 us -> 0.02 us
    dot_general x14 -> x0, matrix products: 65.9 us -> none  [the longest x5 25.8 us: narrow_product(): jnp.einsum(pattern, former, latter, preferred_element_type=jnp.float32)]
    all_gather x1, waiting for transfers between devices: 37.8 us -> 0.01 us  [body(): w_all = lax.all_gather(out_proj.astype(bf16), 'x', axis=0, tiled=True)]
    ppermute x0 -> x24, starting transfers between devices: none -> 28.7 us  [the longest x18 27.6 us: shifted(): lax.ppermute(value, axis, [(i, (i + by) % size) for i in range(size)])]
    all_gather x1 -> x0, blocking collectives: 24.8 us -> none  [sent_together(): lax.all_gather(both, axis, axis=dim, tiled=True)]
    pallas_call x0 -> x6, Pallas kernels: none -> 23.8 us  [the longest x1 11.9 us: body(): kernel_call(segment_kernel, (whole((PADDED, WIDTH), f32), whole((KEYS, 2...]
    ppermute x0 -> x24, waiting for transfers between devices: none -> 13.7 us  [the longest x18 11.2 us: shifted(): lax.ppermute(value, axis, [(i, (i + by) % size) for i in range(size)])]
    another operation x1 -> x2, other arithmetic: 10.3 us -> 1.28 us
  transfers between devices with their start and end apart: 5 -> 27, of which waited for: 4 -> 11; matrix products, arithmetic and copies ran while one was open for 26% -> 8% of each run, Pallas kernels for 0% -> 16%
where the time goes in v1:
time: 126 us; the launch traced here: 125 us
  starting transfers between devices  40.9 us (32%)
  waiting for transfers between devices  29.5 us (23%)
  Pallas kernels  23.8 us (19%)
  between operations  14.4 us (11%)
  local copies, waits for them, and re-layouts  9.51 us (8%)
  other arithmetic  7.12 us (6%)
    ppermute x18, starting transfers between devices, shifted(): lax.ppermute(value, axis, [(i, (i + by) % size) for i in range(size)])  27.6 us
    pallas_call x1, Pallas kernels, body(): kernel_call(segment_kernel, (whole((PADDED, WIDTH), f32), whole((KEYS, 2...  11.9 us
    ppermute x18, waiting for transfers between devices, shifted(): lax.ppermute(value, axis, [(i, (i + by) % size) for i in range(size)])  11.2 us
    all_to_all x1, waiting for transfers between devices, body(): lax.all_to_all(sent, STRETCH, 0, 0, tiled=True).reshape(KEYS, 2 * WIDTH)  9.76 us
    all_to_all x1, starting transfers between devices, body(): lax.all_to_all(sent, STRETCH, 0, 0, tiled=True).reshape(KEYS, 2 * WIDTH)  7.25 us
    all_to_all x1, waiting for transfers between devices, body(): lax.all_to_all(pieces, STRETCH, 0, 0, tiled=True).astype(f32).sum(axis=0)  6.08 us
    unnamed x41, local copies, waits for them, and re-layouts  5.12 us
    all_to_all x1, starting transfers between devices, body(): lax.all_to_all(pieces, STRETCH, 0, 0, tiled=True).astype(f32).sum(axis=0)  4.89 us
  transfers between devices with their start and end apart: 27, of which 11 were waited for; matrix products, arithmetic and copies ran while one was open for 8% of the time, Pallas kernels for 16%

profile of v1, /device:TPU:0, one launch (start us, length us, event | category | flops | bytes accessed | tf_op | source)
XLA Modules:
  0.0 125.2 jit_solution(16708646550549737082)
XLA Ops:
  7.2 0.0 all-gather.2.cloned.1.call-start
  7.2 1.8 %convert_element_type.48 = bf16[256,512]{1,0:T(8,128)(2,1)} convert(f32[256,512]{1,0:T(8,128)} %param.17) | non-fusion elementwise | flops 131072 | bytes 786432 | tf_op jit(solution)/shard_map/convert_element_type | solution.py:247
  9.0 0.0 all-gather.2.cloned.1.call-update
  9.1 0.7 fusion.15
  9.8 0.8 broadcast_in_dim.2
  10.6 7.2 %all-to-all-start = ((bf16[16,48,256]{2,1,0:T(8,128)(2,1)}), bf16[16,48,256]{2,1,0:T(8,128)(2,1)S(1)}, u32[]{:S(2)}, u32[]{:S(2)}) async-start(bf16[16,48,256]{2,1,0:T(8,128)(2,1)} %broadcast_in_dim.2), calls=%async_computation | async-start | bytes 786432 | tf_op jit(solution)/shard_map/all_to_all | solution.py:254
  17.9 9.8 %all-to-all-done = bf16[16,48,256]{2,1,0:T(8,128)(2,1)S(1)} async-done(((bf16[16,48,256]{2,1,0:T(8,128)(2,1)}), bf16[16,48,256]{2,1,0:T(8,128)(2,1)S(1)}, u32[]{:S(2)}, u32[]{:S(2)}) %all-to-all-start) | async-done | bytes 393248 | tf_op jit(solution)/shard_map/all_to_all | solution.py:254
  27.7 2.7 %shard_map.120 = (f32[768,512]{1,0:T(8,128)S(1)}, bf16[128,512]{1,0:T(8,128)(2,1)S(1)}) custom-call(s32[1,512]{1,0:T(1,128)S(1)} %bitcast.67, f32[512,128]{1,0:T(8,128)S(1)} %bitcast.63, bf16[768,256]{1,0:T(8,128)(2,1)S(1)} %bitcast.60), custom_call_target="tpu_custom_call" | custom-call | flops 503316480 | bytes 3145728 | tf_op jit(solution)/shard_map/pallas_call | solution.py:271
  30.3 0.4 collective-permute-start
  30.7 2.1 %collective-permute-start.1 = (bf16[128,512]{1,0:T(8,128)(2,1)S(1)}, bf16[128,512]{1,0:T(8,128)(2,1)S(1)}, u32[]{:S(2)}, u32[]{:S(2)}) collective-permute-start(bf16[128,512]{1,0:T(8,128)(2,1)S(1)} %get-tuple-element.36.a_0), channel_id=1, source_target_pairs={{0,16},{8,24},{16,0},{24,8},{1,17},{9,25},{17,1},{25,9},{2,18},{10... | collective-permute-start | bytes 393224 | tf_op jit(solution)/shard_map/ppermute | solution.py:52
  32.8 1.7 %collective-permute-start.2 = (bf16[128,512]{1,0:T(8,128)(2,1)S(1)}, bf16[128,512]{1,0:T(8,128)(2,1)S(1)}, u32[]{:S(2)}, u32[]{:S(2)}) collective-permute-start(bf16[128,512]{1,0:T(8,128)(2,1)S(1)} %get-tuple-element.36.a_0), channel_id=1, source_target_pairs={{0,24},{8,0},{16,8},{24,16},{1,25},{9,1},{17,9},{25,17},{2,26},{10... | collective-permute-start | bytes 393224 | tf_op jit(solution)/shard_map/ppermute | solution.py:52
  34.5 0.9 reshape.85
  35.4 0.1 pad_add_fusion.place
  35.4 2.7 %collective-permute-done.a_1 = bf16[128,512]{1,0:T(8,128)(2,1)S(1)} collective-permute-done((bf16[128,512]{1,0:T(8,128)(2,1)S(1)}, bf16[128,512]{1,0:T(8,128)(2,1)S(1)}, u32[]{:S(2)}, u32[]{:S(2)}) %collective-permute-start) | collective-permute-done | bytes 131104 | tf_op jit(solution)/shard_map/ppermute | solution.py:52
  38.1 0.7 copy-done.6
  38.8 0.7 copy-done.9
  39.5 1.2 copy-done
  40.7 0.9 copy-done.7
  41.6 0.9 copy-done.10
  42.5 2.6 %shard_map.121 = (f32[4,512,128]{2,1,0:T(8,128)S(1)}, bf16[4,512,128]{2,1,0:T(8,128)(2,1)}) custom-call(s32[4]{0:T(128)S(1)} %pad_add_fusion.place, bf16[128,512]{1,0:T(8,128)(2,1)S(1)} %get-tuple-element.36.a_0, bf16[128,512]{1,0:T(8,128)(2,1)S(1)} %collective-permute-done.a_1, bf16[128,512]{1,0:T(8,128)(2,1)S(1)} %copy-done.7, ...), custom_call_target="tpu_custom_call" | custom-call | flops 536870912 | bytes 3145728 | tf_op jit(solution)/shard_map/pallas_call | solution.py:301
  45.1 0.9 constant_dynamic-slice_fusion.1
  46.0 0.7 copy.26
  46.7 0.5 collective-permute-start.4
  47.2 1.3 %collective-permute-done.4 = f32[2,128,128]{2,1,0:T(8,128)} collective-permute-done((f32[2,128,128]{2,1,0:T(8,128)}, f32[2,128,128]{2,1,0:T(8,128)}, u32[]{:S(2)}, u32[]{:S(2)}) %collective-permute-start.4) | collective-permute-done | bytes 131104 | tf_op jit(solution)/shard_map/ppermute | solution.py:258
  48.5 1.0 fusion.5
  49.5 0.1 fusion.10
  49.6 0.9 collective-permute-start.5
  50.5 1.2 fusion.16
  51.7 0.0 copy-start.15
  51.8 4.6 %collective-permute-start.10 = (bf16[512,128]{1,0:T(8,128)(2,1)S(1)}, bf16[512,128]{1,0:T(8,128)(2,1)S(1)}, u32[]{:S(2)}, u32[]{:S(2)}) collective-permute-start(bf16[512,128]{1,0:T(8,128)(2,1)S(1)} %get-tuple-element.59), channel_id=1, source_target_pairs={{0,6},{2,0},{4,2},{6,4},{1,7},{3,1},{5,3},{7,5},{8,14},{10,8},{12,... | collective-permute-start | bytes 393224 | tf_op jit(solution)/shard_map/ppermute | solution.py:52
  56.4 1.5 %collective-permute-start.9 = (bf16[512,128]{1,0:T(8,128)(2,1)S(1)}, bf16[512,128]{1,0:T(8,128)(2,1)S(1)}, u32[]{:S(2)}, u32[]{:S(2)}) collective-permute-start(bf16[512,128]{1,0:T(8,128)(2,1)S(1)} %get-tuple-element.60), channel_id=1, source_target_pairs={{0,4},{2,6},{4,0},{6,2},{1,5},{3,7},{5,1},{7,3},{8,12},{10,14},{12... | collective-permute-start | bytes 393224 | tf_op jit(solution)/shard_map/ppermute | solution.py:52
  57.9 3.1 %collective-permute-start.6 = (f32[128,128]{1,0:T(8,128)S(1)}, f32[128,128]{1,0:T(8,128)S(1)}, u32[]{:S(2)}, u32[]{:S(2)}) collective-permute-start(f32[128,128]{1,0:T(8,128)S(1)} %get-tuple-element.65), channel_id=1, source_target_pairs={{0,16},{8,24},{16,0},{24,8},{1,17},{9,25},{17,1},{25,9},{2,18},{10... | collective-permute-start | bytes 196616 | tf_op jit(solution)/shard_map/ppermute | solution.py:52
  61.1 0.1 collective-permute-start.7
  61.2 2.5 %collective-permute-done.6 = f32[128,128]{1,0:T(8,128)S(1)} collective-permute-done((f32[128,128]{1,0:T(8,128)S(1)}, f32[128,128]{1,0:T(8,128)S(1)}, u32[]{:S(2)}, u32[]{:S(2)}) %collective-permute-start.6) | collective-permute-done | bytes 65568 | tf_op jit(solution)/shard_map/ppermute | solution.py:52
  63.7 1.6 %collective-permute-done.7 = f32[128,128]{1,0:T(8,128)S(1)} collective-permute-done((f32[128,128]{1,0:T(8,128)S(1)}, f32[128,128]{1,0:T(8,128)S(1)}, u32[]{:S(2)}, u32[]{:S(2)}) %collective-permute-start.7) | collective-permute-done | bytes 65568 | tf_op jit(solution)/shard_map/ppermute | solution.py:52
  65.3 0.3 collective-permute-done.8
  65.6 0.1 fusion.4.e_0
  65.7 2.1 %collective-permute-start.11 = (bf16[512,128]{1,0:T(8,128)(2,1)S(1)}, bf16[512,128]{1,0:T(8,128)(2,1)S(1)}, u32[]{:S(2)}, u32[]{:S(2)}) collective-permute-start(bf16[512,128]{1,0:T(8,128)(2,1)S(1)} %fusion.4.e_0), channel_id=1, source_target_pairs={{0,2},{2,4},{4,6},{6,0},{1,3},{3,5},{5,7},{7,1},{8,10},{10,12},{12... | collective-permute-start | bytes 393224 | tf_op jit(solution)/shard_map/ppermute | solution.py:52
  67.7 0.6 collective-permute-start.12
  68.3 2.2 %collective-permute-start.13 = (bf16[512,128]{1,0:T(8,128)(2,1)S(1)}, bf16[512,128]{1,0:T(8,128)(2,1)S(1)}, u32[]{:S(2)}, u32[]{:S(2)}) collective-permute-start(bf16[512,128]{1,0:T(8,128)(2,1)S(1)} %fusion.4.e_0), channel_id=1, source_target_pairs={{0,6},{2,0},{4,2},{6,4},{1,7},{3,1},{5,3},{7,5},{8,14},{10,8},{12,... | collective-permute-start | bytes 393224 | tf_op jit(solution)/shard_map/ppermute | solution.py:52
  70.5 4.1 %collective-permute-done.11.e_1 = bf16[512,128]{1,0:T(8,128)(2,1)S(1)} collective-permute-done((bf16[512,128]{1,0:T(8,128)(2,1)S(1)}, bf16[512,128]{1,0:T(8,128)(2,1)S(1)}, u32[]{:S(2)}, u32[]{:S(2)}) %collective-permute-start.11) | collective-permute-done | bytes 131104 | tf_op jit(solution)/shard_map/ppermute | solution.py:52
  74.6 0.5 collective-permute-start.16
  75.1 0.1 collective-permute-start.17
  75.2 0.0 copy-start.13
  75.2 0.0 copy-start.14
  75.4 0.6 collective-permute-done.15.o_1
  75.9 0.2 collective-permute-done.16.o_2
  76.1 0.3 collective-permute-done.17.o_3
  76.5 1.3 %shard_map.122 = (f32[128,512]{1,0:T(8,128)S(1)}, bf16[128,512]{1,0:T(8,128)(2,1)S(1)}, bf16[128,512]{1,0:T(8,128)(2,1)S(1)}, bf16[128,512]{1,0:T(8,128)(2,1)S(1)}) custom-call(s32[4]{0:T(128)S(1)} %pad_add_fusion.place, bf16[512,128]{1,0:T(8,128)(2,1)S(1)} %fusion.4.e_0, bf16[512,128]{1,0:T(8,128)(2,1)S(1)} %collective-permute-done.11.e_1, ...), custom_call_target="tpu_custom_call" | custom-call | flops 536870912 | bytes 3145728 | tf_op jit(solution)/shard_map/pallas_call | solution.py:320
  77.8 2.0 %collective-permute-start.18 = (bf16[128,512]{1,0:T(8,128)(2,1)S(1)}, bf16[128,512]{1,0:T(8,128)(2,1)S(1)}, u32[]{:S(2)}, u32[]{:S(2)}) collective-permute-start(bf16[128,512]{1,0:T(8,128)(2,1)S(1)} %get-tuple-element.40), channel_id=1, source_target_pairs={{0,24},{8,0},{16,8},{24,16},{1,25},{9,1},{17,9},{25,17},{2,26},{10... | collective-permute-start | bytes 393224 | tf_op jit(solution)/shard_map/ppermute | solution.py:52
  79.9 2.1 %shard_map.124 = (bf16[256,512]{1,0:T(8,128)(2,1)S(1)}, bf16[256,512]{1,0:T(8,128)(2,1)}, bf16[256,512]{1,0:T(8,128)(2,1)}, bf16[256,512]{1,0:T(8,128)(2,1)}) custom-call(s32[4]{0:T(128)S(1)} %pad_add_fusion.place, bf16[512,128]{1,0:T(8,128)(2,1)S(1)} %fusion.4.e_0, bf16[512,128]{1,0:T(8,128)(2,1)S(1)} %collective-permute-done.11.e_1, ...), custom_call_target="tpu_custom_call" | custom-call | flops 536870912 | bytes 3145728 | tf_op jit(solution)/shard_map/pallas_call | solution.py:331
  82.0 0.3 collective-permute-start.21
  82.3 3.0 %collective-permute-start.22 = (bf16[256,512]{1,0:T(8,128)(2,1)}, bf16[256,512]{1,0:T(8,128)(2,1)}, u32[]{:S(2)}, u32[]{:S(2)}) collective-permute-start(bf16[256,512]{1,0:T(8,128)(2,1)} %get-tuple-element.49), channel_id=1, source_target_pairs={{0,64},{32,96},{64,0},{96,32},{1,65},{33,97},{65,1},{97,33},{2,66}... | collective-permute-start | bytes 786440 | tf_op jit(solution)/shard_map/ppermute | solution.py:52
  85.3 0.7 collective-permute-start.23
  86.0 0.9 collective-permute-start.19
  86.9 1.4 %collective-permute-start.20 = (bf16[128,512]{1,0:T(8,128)(2,1)S(1)}, bf16[128,512]{1,0:T(8,128)(2,1)S(1)}, u32[]{:S(2)}, u32[]{:S(2)}) collective-permute-start(bf16[128,512]{1,0:T(8,128)(2,1)S(1)} %get-tuple-element.42), channel_id=1, source_target_pairs={{0,8},{8,16},{16,24},{24,0},{1,9},{9,17},{17,25},{25,1},{2,10},{10... | collective-permute-start | bytes 393224 | tf_op jit(solution)/shard_map/ppermute | solution.py:52
  88.3 11.9 %shard_map.119 = (f32[1792,128]{1,0:T(8,128)S(1)}, f32[768,256]{1,0:T(8,128)S(1)}, f32[432,256]{1,0:T(8,128)S(1)}) custom-call(s32[4]{0:T(128)S(1)} %pad_add_fusion.place, bf16[1792,128]{1,0:T(8,128)(2,1)S(1)} %pad.9.q, bf16[1792,128]{1,0:T(8,128)(2,1)S(1)} %pad.10.d, bf16[768,256]{1,0:T(8,128)(2,1)S(1)} %bitcast.61, bf16[432,256]{1,0:T(8,128)(2,1)S(1)} %pad_maximum_fusion.own_kv), custom_call_target="tpu_custom_call" | custom-call | flops 2752512000 | bytes 4194304 | tf_op jit(solution)/shard_map/pallas_call | solution.py:285
  100.2 3.3 %shard_map.123 = (f32[128,4,128]{2,1,0:T(4,128)}, bf16[768,256]{1,0:T(8,128)(2,1)}) custom-call(f32[128,512]{1,0:T(8,128)S(1)} %get-tuple-element.39.g_0, bf16[128,512]{1,0:T(8,128)(2,1)S(1)} %collective-permute-done.18.g_1, bf16[128,512]{1,0:T(8,128)(2,1)S(1)} %collective-permute-done.19.g_2, bf16[128,512]{1,0:T(8,128)(2,1)S(1)} %collective-permute-done.20.g_3, ...), custom_call_target="tpu_custom_call" | custom-call | flops 805306368 | bytes 5242880 | tf_op jit(solution)/shard_map/pallas_call | solution.py:343
  103.5 4.9 %all-to-all-start.1 = ((bf16[16,48,256]{2,1,0:T(8,128)(2,1)}), bf16[16,48,256]{2,1,0:T(8,128)(2,1)S(1)}, u32[]{:S(2)}, u32[]{:S(2)}) async-start(bf16[16,48,256]{2,1,0:T(8,128)(2,1)} %bitcast.27), calls=%async_computation.1 | async-start | bytes 786432 | tf_op jit(solution)/shard_map/all_to_all | solution.py:353
  108.4 1.0 slice.47
  109.4 2.1 %convert_add_fusion.1 = f32[256,512]{1,0:T(8,128)} fusion(bf16[256,512]{1,0:T(8,128)(2,1)} %collective-permute-done.23, bf16[256,512]{1,0:T(8,128)(2,1)} %collective-permute-done.22, bf16[256,512]{1,0:T(8,128)(2,1)} %collective-permute-done.21, bf16[256,512]{1,0:T(8,128)(2,1)S(1)} %get-tuple-element.47), kind=kLoop, calls=%fused_computation.2 | loop fusion | flops 917504 | bytes 1572864 | tf_op jit(solution)/shard_map/add | solution.py:341
  111.4 6.1 %all-to-all-done.1 = bf16[16,48,256]{2,1,0:T(8,128)(2,1)S(1)} async-done(((bf16[16,48,256]{2,1,0:T(8,128)(2,1)}), bf16[16,48,256]{2,1,0:T(8,128)(2,1)S(1)}, u32[]{:S(2)}, u32[]{:S(2)}) %all-to-all-start.1) | async-done | bytes 393248 | tf_op jit(solution)/shard_map/all_to_all | solution.py:353
  117.5 0.1 convert_reduce_fusion
  117.6 0.8 fusion.17
  (60 shorter events, 0.3 us)
Async XLA Ops:
  7.2 10.7 %copy-start.17 = (f32[128,4,128]{2,1,0:T(4,128)S(1)}, f32[128,4,128]{2,1,0:T(4,128)}, u32[]{:S(2)}) copy-start(f32[128,4,128]{2,1,0:T(4,128)} %param.14) | copy-start | bytes 786436
  7.2 10.7 %copy-start.19 = (s32[128]{0:T(128)S(1)}, s32[128]{0:T(128)}, u32[]{:S(2)}) copy-start(s32[128]{0:T(128)} %param.15) | copy-start | bytes 1540
  7.2 32.3 %all-gather.2.cloned.1.call-start = ((), (), s32[]{:S(2)}) async-start(), calls=%async_computation.2 | async-start | bytes 1310720 | tf_op jit(solution)/shard_map/all_gather | solution.py:247
  10.6 23.9 %copy-start.18 = (f32[128,512]{1,0:T(8,128)S(1)}, f32[128,512]{1,0:T(8,128)}, u32[]{:S(2)}) copy-start(f32[128,512]{1,0:T(8,128)} %param.16) | copy-start | bytes 786436
  10.6 17.1 %all-to-all-start = ((bf16[16,48,256]{2,1,0:T(8,128)(2,1)}), bf16[16,48,256]{2,1,0:T(8,128)(2,1)S(1)}, u32[]{:S(2)}, u32[]{:S(2)}) async-start(bf16[16,48,256]{2,1,0:T(8,128)(2,1)} %broadcast_in_dim.2), calls=%async_computation | async-start | bytes 786432 | tf_op jit(solution)/shard_map/all_to_all | solution.py:254
  30.3 7.8 %collective-permute-start = (bf16[128,512]{1,0:T(8,128)(2,1)S(1)}, bf16[128,512]{1,0:T(8,128)(2,1)S(1)}, u32[]{:S(2)}, u32[]{:S(2)}) collective-permute-start(bf16[128,512]{1,0:T(8,128)(2,1)S(1)} %get-tuple-element.36.a_0), channel_id=1, source_target_pairs={{0,8},{8,16},{16,24},{24,0},{1,9},{9,17},{17,25},{25,1},{2,10},{10... | collective-permute-start | bytes 393224 | tf_op jit(solution)/shard_map/ppermute | solution.py:52
  30.7 7.4 %collective-permute-start.1 = (bf16[128,512]{1,0:T(8,128)(2,1)S(1)}, bf16[128,512]{1,0:T(8,128)(2,1)S(1)}, u32[]{:S(2)}, u32[]{:S(2)}) collective-permute-start(bf16[128,512]{1,0:T(8,128)(2,1)S(1)} %get-tuple-element.36.a_0), channel_id=1, source_target_pairs={{0,16},{8,24},{16,0},{24,8},{1,17},{9,25},{17,1},{25,9},{2,18},{10... | collective-permute-start | bytes 393224 | tf_op jit(solution)/shard_map/ppermute | solution.py:52
  32.8 6.0 %collective-permute-start.2 = (bf16[128,512]{1,0:T(8,128)(2,1)S(1)}, bf16[128,512]{1,0:T(8,128)(2,1)S(1)}, u32[]{:S(2)}, u32[]{:S(2)}) collective-permute-start(bf16[128,512]{1,0:T(8,128)(2,1)S(1)} %get-tuple-element.36.a_0), channel_id=1, source_target_pairs={{0,24},{8,0},{16,8},{24,16},{1,25},{9,1},{17,9},{25,17},{2,26},{10... | collective-permute-start | bytes 393224 | tf_op jit(solution)/shard_map/ppermute | solution.py:52
  38.1 11.4 %copy-start.4 = (bf16[128,512]{1,0:T(8,128)(2,1)}, bf16[128,512]{1,0:T(8,128)(2,1)S(1)}, u32[]{:S(2)}) copy-start(bf16[128,512]{1,0:T(8,128)(2,1)S(1)} %collective-permute-done.a_1) | copy-start | bytes 393220
  38.1 0.7 copy-start.6
  38.8 0.7 copy-start.9
  39.5 1.2 copy-start
  40.7 0.9 copy-start.7
  41.6 0.9 copy-start.10
  42.5 2.6 %copy-start.12 = (f32[128,2,2,128]{3,2,1,0:T(2,128)S(1)}, f32[128,2,2,128]{3,2,1,0:T(2,128)}, u32[]{:S(2)}) copy-start(f32[128,2,2,128]{3,2,1,0:T(2,128)} %reshape.85) | copy-start | bytes 786436
  45.1 5.4 %collective-permute-start.3 = (bf16[4,512,128]{2,1,0:T(8,128)(2,1)}, bf16[4,512,128]{2,1,0:T(8,128)(2,1)}, u32[]{:S(2)}, u32[]{:S(2)}) collective-permute-start(bf16[4,512,128]{2,1,0:T(8,128)(2,1)} %get-tuple-element.38), channel_id=1, source_target_pairs={{0,1},{1,0},{2,3},{3,2},{4,5},{5,4},{6,7},{7,6},{8,9},{9,8},{10,11... | collective-permute-start | bytes 1572872 | tf_op jit(solution)/shard_map/ppermute | solution.py:308
  46.7 1.8 %collective-permute-start.4 = (f32[2,128,128]{2,1,0:T(8,128)}, f32[2,128,128]{2,1,0:T(8,128)}, u32[]{:S(2)}, u32[]{:S(2)}) collective-permute-start(f32[2,128,128]{2,1,0:T(8,128)} %bitcast.59), channel_id=1, source_target_pairs={{0,1},{1,0},{2,3},{3,2},{4,5},{5,4},{6,7},{7,6},{8,9},{9,8},{10,11... | collective-permute-start | bytes 393224 | tf_op jit(solution)/shard_map/ppermute | solution.py:258
  49.6 11.5 %collective-permute-start.5 = (f32[128,128]{1,0:T(8,128)S(1)}, f32[128,128]{1,0:T(8,128)S(1)}, u32[]{:S(2)}, u32[]{:S(2)}) collective-permute-start(f32[128,128]{1,0:T(8,128)S(1)} %get-tuple-element.64), channel_id=1, source_target_pairs={{0,8},{8,16},{16,24},{24,0},{1,9},{9,17},{17,25},{25,1},{2,10},{10... | collective-permute-start | bytes 196616 | tf_op jit(solution)/shard_map/ppermute | solution.py:52
  51.7 23.5 %copy-start.15 = (bf16[1,432,4,128]{3,2,1,0:T(4,128)(2,1)S(1)}, bf16[1,432,4,128]{3,2,1,0:T(4,128)(2,1)}, u32[]{:S(2)}) copy-start(bf16[1,432,4,128]{3,2,1,0:T(4,128)(2,1)} %param.13) | copy-start | bytes 1327108
  51.8 23.5 %copy-start.16 = (bf16[1,432,4,128]{3,2,1,0:T(4,128)(2,1)S(1)}, bf16[1,432,4,128]{3,2,1,0:T(4,128)(2,1)}, u32[]{:S(2)}) copy-start(bf16[1,432,4,128]{3,2,1,0:T(4,128)(2,1)} %param.10) | copy-start | bytes 1327108
  51.8 24.7 %copy-start.1 = (bf16[1024,512]{1,0:T(8,128)(2,1)S(1)}, bf16[1024,512]{1,0:T(8,128)(2,1)}, u32[]{:S(2)}) copy-start(bf16[1024,512]{1,0:T(8,128)(2,1)} %all-gather.2.cloned.1.call-done) | copy-start | bytes 3145732
  51.8 13.5 %collective-permute-start.10 = (bf16[512,128]{1,0:T(8,128)(2,1)S(1)}, bf16[512,128]{1,0:T(8,128)(2,1)S(1)}, u32[]{:S(2)}, u32[]{:S(2)}) collective-permute-start(bf16[512,128]{1,0:T(8,128)(2,1)S(1)} %get-tuple-element.59), channel_id=1, source_target_pairs={{0,6},{2,0},{4,2},{6,4},{1,7},{3,1},{5,3},{7,5},{8,14},{10,8},{12,... | collective-permute-start | bytes 393224 | tf_op jit(solution)/shard_map/ppermute | solution.py:52
  56.4 9.2 %collective-permute-start.8 = (bf16[512,128]{1,0:T(8,128)(2,1)S(1)}, bf16[512,128]{1,0:T(8,128)(2,1)S(1)}, u32[]{:S(2)}, u32[]{:S(2)}) collective-permute-start(bf16[512,128]{1,0:T(8,128)(2,1)S(1)} %get-tuple-element.58), channel_id=1, source_target_pairs={{0,2},{2,4},{4,6},{6,0},{1,3},{3,5},{5,7},{7,1},{8,10},{10,12},{12... | collective-permute-start | bytes 393224 | tf_op jit(solution)/shard_map/ppermute | solution.py:52
  56.4 9.2 %collective-permute-start.9 = (bf16[512,128]{1,0:T(8,128)(2,1)S(1)}, bf16[512,128]{1,0:T(8,128)(2,1)S(1)}, u32[]{:S(2)}, u32[]{:S(2)}) collective-permute-start(bf16[512,128]{1,0:T(8,128)(2,1)S(1)} %get-tuple-element.60), channel_id=1, source_target_pairs={{0,4},{2,6},{4,0},{6,2},{1,5},{3,7},{5,1},{7,3},{8,12},{10,14},{12... | collective-permute-start | bytes 393224 | tf_op jit(solution)/shard_map/ppermute | solution.py:52
  57.9 5.8 %collective-permute-start.6 = (f32[128,128]{1,0:T(8,128)S(1)}, f32[128,128]{1,0:T(8,128)S(1)}, u32[]{:S(2)}, u32[]{:S(2)}) collective-permute-start(f32[128,128]{1,0:T(8,128)S(1)} %get-tuple-element.65), channel_id=1, source_target_pairs={{0,16},{8,24},{16,0},{24,8},{1,17},{9,25},{17,1},{25,9},{2,18},{10... | collective-permute-start | bytes 196616 | tf_op jit(solution)/shard_map/ppermute | solution.py:52
  61.1 4.3 %collective-permute-start.7 = (f32[128,128]{1,0:T(8,128)S(1)}, f32[128,128]{1,0:T(8,128)S(1)}, u32[]{:S(2)}, u32[]{:S(2)}) collective-permute-start(f32[128,128]{1,0:T(8,128)S(1)} %get-tuple-element.66), channel_id=1, source_target_pairs={{0,24},{8,0},{16,8},{24,16},{1,25},{9,1},{17,9},{25,17},{2,26},{10... | collective-permute-start | bytes 196616 | tf_op jit(solution)/shard_map/ppermute | solution.py:52
  65.7 8.9 %collective-permute-start.11 = (bf16[512,128]{1,0:T(8,128)(2,1)S(1)}, bf16[512,128]{1,0:T(8,128)(2,1)S(1)}, u32[]{:S(2)}, u32[]{:S(2)}) collective-permute-start(bf16[512,128]{1,0:T(8,128)(2,1)S(1)} %fusion.4.e_0), channel_id=1, source_target_pairs={{0,2},{2,4},{4,6},{6,0},{1,3},{3,5},{5,7},{7,1},{8,10},{10,12},{12... | collective-permute-start | bytes 393224 | tf_op jit(solution)/shard_map/ppermute | solution.py:52
  67.7 6.9 %collective-permute-start.12 = (bf16[512,128]{1,0:T(8,128)(2,1)S(1)}, bf16[512,128]{1,0:T(8,128)(2,1)S(1)}, u32[]{:S(2)}, u32[]{:S(2)}) collective-permute-start(bf16[512,128]{1,0:T(8,128)(2,1)S(1)} %fusion.4.e_0), channel_id=1, source_target_pairs={{0,4},{2,6},{4,0},{6,2},{1,5},{3,7},{5,1},{7,3},{8,12},{10,14},{12... | collective-permute-start | bytes 393224 | tf_op jit(solution)/shard_map/ppermute | solution.py:52
  68.3 6.8 %collective-permute-start.13 = (bf16[512,128]{1,0:T(8,128)(2,1)S(1)}, bf16[512,128]{1,0:T(8,128)(2,1)S(1)}, u32[]{:S(2)}, u32[]{:S(2)}) collective-permute-start(bf16[512,128]{1,0:T(8,128)(2,1)S(1)} %fusion.4.e_0), channel_id=1, source_target_pairs={{0,6},{2,0},{4,2},{6,4},{1,7},{3,1},{5,3},{7,5},{8,14},{10,8},{12,... | collective-permute-start | bytes 393224 | tf_op jit(solution)/shard_map/ppermute | solution.py:52
  70.5 4.8 %collective-permute-start.14 = (bf16[512,128]{1,0:T(8,128)(2,1)S(1)}, bf16[512,128]{1,0:T(8,128)(2,1)S(1)}, u32[]{:S(2)}, u32[]{:S(2)}) collective-permute-start(bf16[512,128]{1,0:T(8,128)(2,1)S(1)} %fusion.4.e_0), channel_id=1, source_target_pairs={{0,1},{1,0},{2,3},{3,2},{4,5},{5,4},{6,7},{7,6},{8,9},{9,8},{10,11... | collective-permute-start | bytes 393224 | tf_op jit(solution)/shard_map/ppermute | solution.py:317
  74.6 1.3 %collective-permute-start.15 = (bf16[512,128]{1,0:T(8,128)(2,1)S(1)}, bf16[512,128]{1,0:T(8,128)(2,1)S(1)}, u32[]{:S(2)}, u32[]{:S(2)}) collective-permute-start(bf16[512,128]{1,0:T(8,128)(2,1)S(1)} %collective-permute-done.11.e_1), channel_id=1, source_target_pairs={{0,1},{1,0},{2,3},{3,2},{4,5},{5,4},{6,7},{7,6},{8,9},{9,8},{10,11... | collective-permute-start | bytes 393224 | tf_op jit(solution)/shard_map/ppermute | solution.py:317
  74.6 1.5 %collective-permute-start.16 = (bf16[512,128]{1,0:T(8,128)(2,1)S(1)}, bf16[512,128]{1,0:T(8,128)(2,1)S(1)}, u32[]{:S(2)}, u32[]{:S(2)}) collective-permute-start(bf16[512,128]{1,0:T(8,128)(2,1)S(1)} %collective-permute-done.12.e_2), channel_id=1, source_target_pairs={{0,1},{1,0},{2,3},{3,2},{4,5},{5,4},{6,7},{7,6},{8,9},{9,8},{10,11... | collective-permute-start | bytes 393224 | tf_op jit(solution)/shard_map/ppermute | solution.py:317
  75.1 1.3 %collective-permute-start.17 = (bf16[512,128]{1,0:T(8,128)(2,1)S(1)}, bf16[512,128]{1,0:T(8,128)(2,1)S(1)}, u32[]{:S(2)}, u32[]{:S(2)}) collective-permute-start(bf16[512,128]{1,0:T(8,128)(2,1)S(1)} %collective-permute-done.13.e_3), channel_id=1, source_target_pairs={{0,1},{1,0},{2,3},{3,2},{4,5},{5,4},{6,7},{7,6},{8,9},{9,8},{10,11... | collective-permute-start | bytes 393224 | tf_op jit(solution)/shard_map/ppermute | solution.py:317
  75.2 4.6 %copy-start.13 = (bf16[1,432,1,128]{3,1,2,0:T(8,128)(2,1)S(1)}, bf16[1,432,1,128]{3,1,2,0:T(8,128)(2,1)}, u32[]{:S(2)}) copy-start(bf16[1,432,1,128]{3,1,2,0:T(8,128)(2,1)} %param.11) | copy-start | bytes 331780
  75.2 4.6 %copy-start.14 = (bf16[1,432,1,128]{3,1,2,0:T(8,128)(2,1)S(1)}, bf16[1,432,1,128]{3,1,2,0:T(8,128)(2,1)}, u32[]{:S(2)}) copy-start(bf16[1,432,1,128]{3,1,2,0:T(8,128)(2,1)} %param.12) | copy-start | bytes 331780
  75.3 4.6 %copy-start.5 = (bf16[128,512]{1,0:T(8,128)(2,1)S(1)}, bf16[128,512]{1,0:T(8,128)(2,1)}, u32[]{:S(2)}) copy-start(bf16[128,512]{1,0:T(8,128)(2,1)} %copy-done.4) | copy-start | bytes 393220
  75.3 4.6 %copy-start.8 = (bf16[128,512]{1,0:T(8,128)(2,1)S(1)}, bf16[128,512]{1,0:T(8,128)(2,1)}, u32[]{:S(2)}) copy-start(bf16[128,512]{1,0:T(8,128)(2,1)} %copy-done.6) | copy-start | bytes 393220
  75.3 4.6 %copy-start.11 = (bf16[128,512]{1,0:T(8,128)(2,1)S(1)}, bf16[128,512]{1,0:T(8,128)(2,1)}, u32[]{:S(2)}) copy-start(bf16[128,512]{1,0:T(8,128)(2,1)} %copy-done.9) | copy-start | bytes 393220
  77.8 9.1 %collective-permute-start.18 = (bf16[128,512]{1,0:T(8,128)(2,1)S(1)}, bf16[128,512]{1,0:T(8,128)(2,1)S(1)}, u32[]{:S(2)}, u32[]{:S(2)}) collective-permute-start(bf16[128,512]{1,0:T(8,128)(2,1)S(1)} %get-tuple-element.40), channel_id=1, source_target_pairs={{0,24},{8,0},{16,8},{24,16},{1,25},{9,1},{17,9},{25,17},{2,26},{10... | collective-permute-start | bytes 393224 | tf_op jit(solution)/shard_map/ppermute | solution.py:52
  82.0 27.4 %collective-permute-start.21 = (bf16[256,512]{1,0:T(8,128)(2,1)}, bf16[256,512]{1,0:T(8,128)(2,1)}, u32[]{:S(2)}, u32[]{:S(2)}) collective-permute-start(bf16[256,512]{1,0:T(8,128)(2,1)} %get-tuple-element.48), channel_id=1, source_target_pairs={{0,32},{32,64},{64,96},{96,0},{1,33},{33,65},{65,97},{97,1},{2,34}... | collective-permute-start | bytes 786440 | tf_op jit(solution)/shard_map/ppermute | solution.py:52
  82.3 27.1 %collective-permute-start.22 = (bf16[256,512]{1,0:T(8,128)(2,1)}, bf16[256,512]{1,0:T(8,128)(2,1)}, u32[]{:S(2)}, u32[]{:S(2)}) collective-permute-start(bf16[256,512]{1,0:T(8,128)(2,1)} %get-tuple-element.49), channel_id=1, source_target_pairs={{0,64},{32,96},{64,0},{96,32},{1,65},{33,97},{65,1},{97,33},{2,66}... | collective-permute-start | bytes 786440 | tf_op jit(solution)/shard_map/ppermute | solution.py:52
  85.3 24.1 %collective-permute-start.23 = (bf16[256,512]{1,0:T(8,128)(2,1)}, bf16[256,512]{1,0:T(8,128)(2,1)}, u32[]{:S(2)}, u32[]{:S(2)}) collective-permute-start(bf16[256,512]{1,0:T(8,128)(2,1)} %get-tuple-element.50), channel_id=1, source_target_pairs={{0,96},{32,0},{64,32},{96,64},{1,97},{33,1},{65,33},{97,65},{2,98}... | collective-permute-start | bytes 786440 | tf_op jit(solution)/shard_map/ppermute | solution.py:52
  86.0 14.2 %collective-permute-start.19 = (bf16[128,512]{1,0:T(8,128)(2,1)S(1)}, bf16[128,512]{1,0:T(8,128)(2,1)S(1)}, u32[]{:S(2)}, u32[]{:S(2)}) collective-permute-start(bf16[128,512]{1,0:T(8,128)(2,1)S(1)} %get-tuple-element.41), channel_id=1, source_target_pairs={{0,16},{8,24},{16,0},{24,8},{1,17},{9,25},{17,1},{25,9},{2,18},{10... | collective-permute-start | bytes 393224 | tf_op jit(solution)/shard_map/ppermute | solution.py:52
  86.9 13.3 %collective-permute-start.20 = (bf16[128,512]{1,0:T(8,128)(2,1)S(1)}, bf16[128,512]{1,0:T(8,128)(2,1)S(1)}, u32[]{:S(2)}, u32[]{:S(2)}) collective-permute-start(bf16[128,512]{1,0:T(8,128)(2,1)S(1)} %get-tuple-element.42), channel_id=1, source_target_pairs={{0,8},{8,16},{16,24},{24,0},{1,9},{9,17},{17,25},{25,1},{2,10},{10... | collective-permute-start | bytes 393224 | tf_op jit(solution)/shard_map/ppermute | solution.py:52
  100.2 3.3 %copy-start.2 = (f32[432,256]{1,0:T(8,128)}, f32[432,256]{1,0:T(8,128)S(1)}, u32[]{:S(2)}) copy-start(f32[432,256]{1,0:T(8,128)S(1)} %get-tuple-element.35) | copy-start | bytes 1327108
  103.5 14.0 %all-to-all-start.1 = ((bf16[16,48,256]{2,1,0:T(8,128)(2,1)}), bf16[16,48,256]{2,1,0:T(8,128)(2,1)S(1)}, u32[]{:S(2)}, u32[]{:S(2)}) async-start(bf16[16,48,256]{2,1,0:T(8,128)(2,1)} %bitcast.27), calls=%async_computation.1 | async-start | bytes 786432 | tf_op jit(solution)/shard_map/all_to_all | solution.py:353
  108.4 9.2 %copy-start.3 = (f32[432,256]{1,0:T(8,128)S(1)}, f32[432,256]{1,0:T(8,128)}, u32[]{:S(2)}) copy-start(f32[432,256]{1,0:T(8,128)} %copy-done.2) | copy-start | bytes 1327108
Sparse Core Ops, SparseCore 0:
  10.3 26.3 all-gather.1

commit v2 on v1

v2 whole, which is shorter than its diff:
```python
import jax
import jax.numpy as jnp
from jax import lax
from jax.experimental import pallas as pl
from jax.experimental.pallas import tpu as pltpu
from jax.sharding import Mesh
from jax.sharding import PartitionSpec as P

SEG_LEN = 384
BEACONS = 48
ITEMS = SEG_LEN + BEACONS
SEGMENTS = 16
HEADS = 4
WIDTH = 128
KEYS = SEGMENTS * BEACONS
READERS = 128
FEATURES = HEADS * WIDTH
SIDE = 4
ROWS = SIDE * READERS
PADDED = 1792
PARTS = ((0, 512), (512, 512), (1024, 384), (1408, 384))
CHUNK = 192
SCALING = WIDTH ** (-0.5)
HIDDEN = -1e30
EXPONENT = SCALING * 1.4426950408889634
CORES = [(0, 1), (1, 0)]
STRETCH = ("x", "y")
HEAD = ("z", "core")

bf16 = jnp.bfloat16
f32 = jnp.float32


def nn(a, b):
    return lax.dot_general(a, b, (((1,), (0,)), ((), ())), preferred_element_type=f32)


def nt(a, b):
    return lax.dot_general(a, b, (((1,), (1,)), ((), ())), preferred_element_type=f32)


def tn(a, b):
    return lax.dot_general(a, b, (((0,), (0,)), ((), ())), preferred_element_type=f32)


def halves(value):
    high = value.astype(bf16)
    return high, (value - high.astype(f32)).astype(bf16)


def shifted(value, axis, by):
    size = lax.axis_size(axis)
    return lax.ppermute(value, axis, [(i, (i + by) % size) for i in range(size)])


VMEM = pl.BlockSpec(memory_space=pltpu.VMEM)
HBM = pl.BlockSpec(memory_space=pltpu.HBM)
SMEM = pl.BlockSpec(memory_space=pltpu.SMEM)


def kernel_call(kernel, ins, outs, scratch=(), limit=16, flops=0, moved=0, aliases={}):
    return pl.pallas_call(
        kernel,
        out_shape=tuple(jax.ShapeDtypeStruct(shape, dtype) for shape, dtype, _ in outs),
        in_specs=list(ins),
        out_specs=tuple(spec for _, _, spec in outs),
        scratch_shapes=list(scratch),
        input_output_aliases=aliases,
        compiler_params=pltpu.CompilerParams(vmem_limit_bytes=limit * 1024 * 1024),
        cost_estimate=pl.CostEstimate(flops=flops, transcendentals=0, bytes_accessed=moved),
    )


def turned(index):
    return lax.rem(index + 2 * SIDE, SIDE)


def segment_kernel(start, count, first):
    own_keys = min((start + count) // HEADS, ITEMS)
    kept = min(count, ITEMS * HEADS - start)
    chunks = [(at, CHUNK) for at in range(0, KEYS, CHUNK)] + [(KEYS, own_keys)]

    def kernel(place, q, d, far_kv, own_kv, *refs):
        dq, far, own, score, grad, dq_rows, done = refs[-7:]
        rows = pl.ds(start, count)
        q_t = q[rows, :]
        d_t = d[rows, :]

        def keys(at, n):
            return far_kv[at : at + n, :WIDTH] if at < KEYS else own_kv[:n, :WIDTH]

        def values(at, n):
            return far_kv[at : at + n, WIDTH:] if at < KEYS else own_kv[:n, WIDTH:]

        top = jnp.full((1, count), HIDDEN, f32)
        for at, n in chunks:
            s = nt(keys(at, n), q_t)
            key = lax.broadcasted_iota(jnp.int32, s.shape, 0)
            if at < KEYS:
                s = jnp.where(key < place[0] * BEACONS - at, s, HIDDEN)
            else:
                item = (lax.broadcasted_iota(jnp.int32, s.shape, 1) + start) >> 2
                s = jnp.where(key <= item, s, HIDDEN)
            score[at : at + n, :] = s
            grad[at : at + n, :] = nt(values(at, n), d_t)
            top = jnp.maximum(top, jnp.max(s, axis=0, keepdims=True))

        bottom = jnp.zeros((1, count), f32)
        total = jnp.zeros((1, count), f32)
        for at, n in chunks:
            e = jnp.exp2((score[at : at + n, :] - top) * EXPONENT)
            score[at : at + n, :] = e
            bottom = bottom + jnp.sum(e, axis=0, keepdims=True)
            total = total + jnp.sum(e * grad[at : at + n, :], axis=0, keepdims=True)
        inverse = 1.0 / bottom
        total = total * inverse

        acc = jnp.zeros((WIDTH, count), f32)
        for at, n in chunks:
            p = score[at : at + n, :] * inverse
            ds = (p * (grad[at : at + n, :] - total)).astype(bf16)
            dk = nn(ds, q_t) * SCALING
            dv = nn(p.astype(bf16), d_t)
            acc = acc + tn(keys(at, n), ds)
            out = far.at[at : at + n] if at < KEYS else own.at[:n]
            if first:
                out[:, :WIDTH] = dk
                out[:, WIDTH:] = dv
            else:
                out[:, :WIDTH] += dk
                out[:, WIDTH:] += dv
        if first:
            own[own_keys:, :] = jnp.zeros((ITEMS - own_keys, 2 * WIDTH), f32)
        dq_rows[...] = (acc * SCALING).T
        copy = pltpu.make_async_copy(
            dq_rows.at[pl.ds(0, kept)], dq.at[pl.ds(start, kept)], done
        )
        copy.start()
        copy.wait()

    return kernel


def target_kernel(place, target, keep, send):
    left = place[2] == 0
    for b in range(2):
        first = target[:, 2 * b * WIDTH : (2 * b + 1) * WIDTH]
        second = target[:, (2 * b + 1) * WIDTH : (2 * b + 2) * WIDTH]
        keep[b] = jnp.where(left, first, second)
        send[b] = jnp.where(left, second, first)


def reader_kernel(place, seen, q, kv, keep, got, probs, a_0, a_1, a_2, a_3, p_scr, done):
    k = kv[:, :WIDTH]
    v = kv[:, WIDTH:]
    outs = (a_0, a_1, a_2, a_3)
    copies = []
    for h in range(0, HEADS, 2):
        cols = pl.ds(h * READERS, 2 * READERS)
        q_all = q[cols, :]
        q_0 = q_all.astype(bf16)
        q_1, q_2 = halves(q_all - q_0.astype(f32))
        s = nt(k, q_0) + nt(k, q_1) + nt(k, q_2)
        key = lax.broadcasted_iota(jnp.int32, s.shape, 0)
        s = jnp.where(key < seen[:, cols], s, HIDDEN)
        e = jnp.exp2((s - jnp.max(s, axis=0, keepdims=True)) * EXPONENT)
        p = e * (1.0 / jnp.sum(e, axis=0, keepdims=True))
        p_scr[h // 2] = p
        copies.append(pltpu.make_async_copy(p_scr.at[h // 2], probs.at[h // 2], done.at[h // 2]))
        copies[-1].start()
        high, low = halves(p)
        out = tn(v, high) + tn(v, low)
        for i in range(2):
            at = (h + i) * WIDTH
            part = out[:, i * READERS : (i + 1) * READERS].T.astype(bf16)
            for a in outs:
                a[:, at : at + WIDTH] = part
    for i, a in enumerate(outs):
        side = lax.rem(place[4] + i, SIDE)
        here = (side >> 1) == place[2]
        t = jnp.where(here, keep[side & 1], got[side & 1])
        high, low = halves(t)
        a[:, FEATURES : FEATURES + WIDTH] = high
        a[:, FEATURES + WIDTH :] = low
    for copy in copies:
        copy.wait()


def beacon_grad_kernel(g_0, g_1, g_2, g_3, probs, q, kv, far, score_grad, beacon_grad, p_scr, done):
    copies = [
        pltpu.make_async_copy(probs.at[i], p_scr.at[i], done.at[i]) for i in range(HEADS // 2)
    ]
    for copy in copies:
        copy.start()
    v = kv[:, WIDTH:]
    dk = jnp.zeros((KEYS, WIDTH), f32)
    dv = far[:, WIDTH:]
    for h in range(0, HEADS, 2):
        cols = pl.ds(h * READERS, 2 * READERS)
        g = []
        for i in range(2):
            at = slice((h + i) * WIDTH, (h + i + 1) * WIDTH)
            g.append(
                g_0[:, at] + g_1[:, at].astype(f32) + g_2[:, at].astype(f32) + g_3[:, at].astype(f32)
            )
        high, low = halves(jnp.concatenate(g, axis=0))
        pg = nt(v, high) + nt(v, low)
        copies[h // 2].wait()
        p = p_scr[h // 2]
        total = jnp.sum(p * pg, axis=0, keepdims=True)
        ds = (p * (pg - total)).astype(bf16)
        score_grad[:, cols] = ds
        dk = dk + nn(ds, q[cols, :].astype(bf16))
        dv = dv + nn(p.astype(bf16), high)
    beacon_grad[:, :WIDTH] = (far[:, :WIDTH] + dk * SCALING).astype(bf16)
    beacon_grad[:, WIDTH:] = dv.astype(bf16)


def query_grad_kernel(score_grad, kv, dq):
    out = tn(kv[:, :WIDTH], score_grad[...]) * SCALING
    for h in range(HEADS):
        dq[:, h, :] = out[:, h * READERS : (h + 1) * READERS].T


def predict_kernel(
    place, a_0, a_1, a_2, a_3, w_0, w_1, w_2, w_3, o_0, o_1, o_2, o_3, other, a_out, w_out, a_scr, w_scr, done
):
    z = place[1]
    left = place[2] == 0
    for i, a in enumerate((a_0, a_1, a_2, a_3)):
        a_scr[i * READERS : (i + 1) * READERS, :] = a[:, :FEATURES]
    for i, w in enumerate((w_0, w_1, w_2, w_3)):
        w_scr[turned(place[3] - i)] = w[...]
    copies = [
        pltpu.make_async_copy(a_scr, a_out, done.at[0]),
        pltpu.make_async_copy(w_scr, w_out, done.at[1]),
    ]
    for copy in copies:
        copy.start()
    for i, own in enumerate((o_0, o_1, o_2, o_3)):
        both = nt(a_scr[...], w_scr[turned(z + i)])
        mine = jnp.where(left, both[:, :WIDTH], both[:, WIDTH:])
        other[i] = jnp.where(left, both[:, WIDTH:], both[:, :WIDTH]).astype(bf16)
        if i == 0:
            for j, a in enumerate((a_0, a_1, a_2, a_3)):
                rows = slice(j * READERS, (j + 1) * READERS)
                high = a[:, FEATURES : FEATURES + WIDTH].astype(f32)
                own[rows, :] = mine[rows] - (high + a[:, FEATURES + WIDTH :].astype(f32))
        else:
            own[...] = mine
    for copy in copies:
        copy.wait()


def chip_sum_kernel(o_0, o_1, o_2, o_3, other, base, c_1, c_2, c_3):
    base[...] = o_0[...] + other[0].astype(f32)
    c_1[...] = (o_1[...] + other[1].astype(f32)).astype(bf16)
    c_2[...] = (o_2[...] + other[2].astype(f32)).astype(bf16)
    c_3[...] = (o_3[...] + other[3].astype(f32)).astype(bf16)


def gather_errors(place, mine, others, errors):
    z = place[1]
    left = place[2] == 0
    for i in range(SIDE):
        at = turned(z - i)
        e = mine[i][...]
        o = others[i][...]
        errors[at, :, :WIDTH] = jnp.where(left, e, o)
        errors[at, :, WIDTH:] = jnp.where(left, o, e)


def attended_grad_kernel(
    place, e_0, e_1, e_2, e_3, o_0, o_1, o_2, o_3, w, g_0, g_1, g_2, g_3, errors, w_scr, done
):
    copy = pltpu.make_async_copy(w, w_scr, done)
    copy.start()
    gather_errors(place, (e_0, e_1, e_2, e_3), (o_0, o_1, o_2, o_3), errors)
    copy.wait()
    for i, out in enumerate((g_0, g_1, g_2, g_3)):
        acc = jnp.zeros((READERS, FEATURES), f32)
        for b in range(SIDE):
            acc = acc + nn(errors[b, i * READERS : (i + 1) * READERS, :], w_scr[b])
        out[...] = acc.astype(out.dtype)


def projection_grad_kernel(
    place, e_0, e_1, e_2, e_3, o_0, o_1, o_2, o_3, a, p_0, p_1, p_2, p_3, errors, a_scr, done
):
    copy = pltpu.make_async_copy(a, a_scr, done)
    copy.start()
    gather_errors(place, (e_0, e_1, e_2, e_3), (o_0, o_1, o_2, o_3), errors)
    copy.wait()
    for i, out in enumerate((p_0, p_1, p_2, p_3)):
        out[...] = tn(errors[turned(place[3] + i)], a_scr[...]).astype(out.dtype)


def items_grad_kernel(own, owned, dk, dv):
    total = jnp.sum(owned[...].astype(f32), axis=0)
    dk[:SEG_LEN, :] = own[:SEG_LEN, :WIDTH]
    dv[:SEG_LEN, :] = own[:SEG_LEN, WIDTH:]
    dk[SEG_LEN:, :] = own[SEG_LEN:, :WIDTH] + total[:, :WIDTH]
    dv[SEG_LEN:, :] = own[SEG_LEN:, WIDTH:] + total[:, WIDTH:]


def body(q_items, k_items, v_items, d_out, reader_query, reader_span, target, out_proj):
    x = lax.axis_index("x")
    y = lax.axis_index("y")
    z = lax.axis_index("z")
    core = lax.axis_index("core")
    place = jnp.stack([x * SIDE + y, z, core, x, y]).astype(jnp.int32)
    together = lax.optimization_barrier
    sems = pltpu.SemaphoreType.DMA
    product = 2 * ROWS * FEATURES * 1024
    reader_product = 2 * KEYS * HEADS * READERS * WIDTH
    megabyte = 1024 * 1024

    own_kv = jnp.concatenate(
        [k_items.reshape(ITEMS, WIDTH), v_items.reshape(ITEMS, WIDTH)], axis=1
    )
    sent = jnp.broadcast_to(own_kv[None, SEG_LEN:], (SEGMENTS, BEACONS, 2 * WIDTH))
    far_kv = lax.all_to_all(sent, STRETCH, 0, 0, tiled=True).reshape(KEYS, 2 * WIDTH)

    w = out_proj.astype(bf16)
    w = [w] + [shifted(w, "x", i) for i in range(1, SIDE)]

    keep, send = kernel_call(
        target_kernel,
        [SMEM, VMEM],
        [((2, READERS, WIDTH), f32, VMEM)] * 2,
        moved=megabyte // 2,
    )(place, target)
    got = lax.ppermute(send, "core", CORES)

    pad = ((0, PADDED - ITEMS * HEADS), (0, 0))
    q_rows = jnp.pad(q_items.reshape(ITEMS * HEADS, WIDTH), pad)
    d_rows = jnp.pad(d_out.reshape(ITEMS * HEADS, WIDTH), pad)
    rq = reader_query.transpose(1, 0, 2).reshape(HEADS * READERS, WIDTH)
    seen = jnp.tile(reader_span * BEACONS, HEADS)[None, :]

    far_kv, keep, got, w, q_rows, d_rows, rq, seen = together(
        (far_kv, keep, got, w, q_rows, d_rows, rq, seen)
    )

    probs, *a = kernel_call(
        reader_kernel,
        [SMEM] + [VMEM] * 5,
        [((HEADS // 2, KEYS, 2 * READERS), f32, HBM)]
        + [((READERS, FEATURES + 2 * WIDTH), bf16, VMEM)] * SIDE,
        scratch=(pltpu.VMEM((HEADS // 2, KEYS, 2 * READERS), f32), sems((HEADS // 2,))),
        flops=5 * reader_product,
        moved=3 * megabyte,
    )(place, seen, rq, far_kv, keep, got)

    sums = []

    def segment_part(i):
        start, count = PARTS[i]
        dq, far, own = kernel_call(
            segment_kernel(start, count, i == 0),
            [SMEM] + [VMEM] * 4 + ([HBM, VMEM, VMEM] if sums else []),
            [
                ((ITEMS * HEADS, WIDTH), f32, HBM),
                ((KEYS, 2 * WIDTH), f32, VMEM),
                ((ITEMS, 2 * WIDTH), f32, VMEM),
            ],
            scratch=(
                pltpu.VMEM((KEYS + ITEMS, count), f32),
                pltpu.VMEM((KEYS + ITEMS, count), f32),
                pltpu.VMEM((count, WIDTH), f32),
                sems,
            ),
            aliases={5: 0, 6: 1, 7: 2} if sums else {},
            limit=24,
            flops=5 * 2 * (KEYS + ITEMS) * count * WIDTH,
            moved=4 * megabyte,
        )(place, q_rows, d_rows, far_kv, own_kv, *sums)
        sums[:] = [dq, far, own]

    q_rows, a[0] = together((q_rows, a[0]))
    a = [a[0]] + [shifted(a[i], "y", i) for i in range(1, SIDE)]
    segment_part(0)
    a, sums[:] = together((a, sums))

    *own, other, a_all, w_all = kernel_call(
        predict_kernel,
        [SMEM] + [VMEM] * 8,
        [((ROWS, WIDTH), f32, VMEM)] * SIDE
        + [
            ((SIDE, ROWS, WIDTH), bf16, VMEM),
            ((ROWS, FEATURES), bf16, HBM),
            ((SIDE, 2 * WIDTH, FEATURES), bf16, HBM),
        ],
        scratch=(
            pltpu.VMEM((ROWS, FEATURES), bf16),
            pltpu.VMEM((SIDE, 2 * WIDTH, FEATURES), bf16),
            sems((2,)),
        ),
        flops=product,
        moved=3 * megabyte,
    )(place, *a, *w)
    from_core = lax.ppermute(other, "core", CORES)
    base, *chip = kernel_call(
        chip_sum_kernel,
        [VMEM] * 5,
        [((ROWS, WIDTH), f32, VMEM)] + [((ROWS, WIDTH), bf16, VMEM)] * (SIDE - 1),
        moved=2 * megabyte,
    )(*own, from_core)
    q_rows, base = together((q_rows, base))
    arrived = [shifted(chip[i - 1], "z", i) for i in range(1, SIDE)]
    segment_part(1)
    arrived, sums[:] = together((arrived, sums))
    for part in arrived:
        base = base + part.astype(f32)
    error = base.astype(bf16)

    q_rows, error = together((q_rows, error))
    mine = [shifted(error, "z", i) for i in range(1, SIDE)]
    segment_part(2)
    mine, sums[:] = together((mine, sums))
    mine = [error] + mine
    others = [lax.ppermute(e, "core", CORES) for e in mine]
    stack = pltpu.VMEM((SIDE, ROWS, 2 * WIDTH), bf16)
    piece = (READERS, FEATURES)
    g = kernel_call(
        attended_grad_kernel,
        [SMEM] + [VMEM] * 8 + [HBM],
        [(piece, f32, VMEM)] + [(piece, bf16, VMEM)] * (SIDE - 1),
        scratch=(stack, pltpu.VMEM((SIDE, 2 * WIDTH, FEATURES), bf16), sems),
        flops=product,
        moved=3 * megabyte,
    )(place, *mine, *others, w_all)
    q_rows, mine[0], g_0 = together((q_rows, mine[0], g[0]))
    g = [g_0] + [shifted(g[i], "y", -i) for i in range(1, SIDE)]

    w_grad = kernel_call(
        projection_grad_kernel,
        [SMEM] + [VMEM] * 8 + [HBM],
        [((2 * WIDTH, FEATURES), f32, VMEM)] + [((2 * WIDTH, FEATURES), bf16, VMEM)] * (SIDE - 1),
        scratch=(stack, pltpu.VMEM((ROWS, FEATURES), bf16), sems),
        flops=product,
        moved=3 * megabyte,
    )(place, *mine, *others, a_all)
    segment_part(3)
    out_proj_grad = w_grad[0]
    for i in range(1, SIDE):
        out_proj_grad = out_proj_grad + shifted(w_grad[i], "x", i).astype(f32)

    q_items_grad, far_grad, own_grad = sums
    score_grad, beacon_grad = kernel_call(
        beacon_grad_kernel,
        [VMEM] * 4 + [HBM] + [VMEM] * 3,
        [((KEYS, HEADS * READERS), bf16, VMEM), ((KEYS, 2 * WIDTH), bf16, VMEM)],
        scratch=(pltpu.VMEM((HEADS // 2, KEYS, 2 * READERS), f32), sems((HEADS // 2,))),
        flops=4 * reader_product,
        moved=5 * megabyte,
    )(*g, probs, rq, far_kv, far_grad)

    pieces = beacon_grad.reshape(SEGMENTS, BEACONS, 2 * WIDTH)
    owned = lax.all_to_all(pieces, STRETCH, 0, 0, tiled=True)
    (reader_query_grad,) = kernel_call(
        query_grad_kernel,
        [VMEM] * 2,
        [((READERS, HEADS, WIDTH), f32, VMEM)],
        flops=reader_product,
        moved=2 * megabyte,
    )(score_grad, far_kv)
    k_items_grad, v_items_grad = kernel_call(
        items_grad_kernel,
        [VMEM] * 2,
        [((ITEMS, WIDTH), f32, VMEM)] * 2,
        moved=megabyte,
    )(own_grad, owned)
    q_items_grad = q_items_grad.reshape(1, ITEMS, HEADS, WIDTH)
    k_items_grad = k_items_grad.reshape(1, ITEMS, 1, WIDTH)
    v_items_grad = v_items_grad.reshape(1, ITEMS, 1, WIDTH)
    return q_items_grad, k_items_grad, v_items_grad, reader_query_grad, out_proj_grad


def solution(mesh):
    axes = Mesh(mesh.devices.reshape(SIDE, SIDE, SIDE, 2), STRETCH + HEAD)
    items = P(STRETCH, None, HEAD, None)
    return jax.shard_map(
        body,
        mesh=axes,
        in_specs=(
            items,
            items,
            items,
            items,
            P(STRETCH, HEAD, None),
            P(STRETCH),
            P(STRETCH, HEAD),
            P(STRETCH, HEAD),
        ),
        out_specs=(items, items, items, P(STRETCH, HEAD, None), P(STRETCH, HEAD)),
        check_vma=False,
    )
```

time: 126 us -> 108 us (0.86)
  between operations: 14.4 us -> 0.93 us
  local copies, waits for them, and re-layouts: 9.51 us -> 3.04 us
  other arithmetic: 7.12 us -> 1.87 us
  Pallas kernels: 23.8 us -> 28.9 us
  starting transfers between devices: 40.9 us -> 42.7 us
    all_to_all x1, waiting for transfers between devices: 9.76 us -> 0.01 us  [body(): lax.all_to_all(sent, STRETCH, 0, 0, tiled=True).reshape(KEYS, 2 * WIDTH)]
    ppermute x18, waiting for transfers between devices: 11.2 us -> 20.2 us  [shifted(): lax.ppermute(value, axis, [(i, (i + by) % size) for i in range(size)])]
    unnamed x41 -> x12, local copies, waits for them, and re-layouts: 5.12 us -> 0.03 us
    pallas_call x6 -> x13, Pallas kernels: 23.8 us -> 28.9 us  [the longest x4 14.4 us: segment_part(): kernel_call(segment_kernel(start, count, i == 0), [SMEM] + [VMEM] * 4 + (...]
    convert_element_type x2, other arithmetic: 1.9 us -> 0.1 us  [the longest x1 0.06 us: body(): error = base.astype(bf16)]
    slice x2 -> x0, local copies, waits for them, and re-layouts: 1.76 us -> none  [the longest x1 0.97 us: body(): q_items_grad = dq_rows[:ITEMS * HEADS].reshape(1, ITEMS, HEADS, WIDTH)]
    ppermute x18, starting transfers between devices: 27.6 us -> 28.9 us  [shifted(): lax.ppermute(value, axis, [(i, (i + by) % size) for i in range(size)])]
    another operation x2 -> x0, other arithmetic: 1.28 us -> none
  transfers between devices with their start and end apart: 27 -> 26, of which waited for: 11 -> 14; matrix products, arithmetic and copies ran while one was open for 8% -> 3% of each run, Pallas kernels for 16% -> 20%
where the time goes in v2:
time: 108 us
  starting transfers between devices  42.7 us (40%)
  waiting for transfers between devices  30.5 us (28%)
  Pallas kernels  28.9 us (27%)
  local copies, waits for them, and re-layouts  3.04 us (3%)
  other arithmetic  1.87 us (2%)
    ppermute x18, starting transfers between devices, shifted(): lax.ppermute(value, axis, [(i, (i + by) % size) for i in range(size)])  28.9 us
    ppermute x18, waiting for transfers between devices, shifted(): lax.ppermute(value, axis, [(i, (i + by) % size) for i in range(size)])  20.2 us
    pallas_call x4, Pallas kernels, segment_part(): kernel_call(segment_kernel(start, count, i == 0), [SMEM] + [VMEM] * 4 + (...  14.4 us
    all_to_all x1, starting transfers between devices, body(): lax.all_to_all(sent, STRETCH, 0, 0, tiled=True).reshape(KEYS, 2 * WIDTH)  7.12 us
    all_to_all x1, waiting for transfers between devices, body(): owned = lax.all_to_all(pieces, STRETCH, 0, 0, tiled=True)  7.01 us
    all_to_all x1, starting transfers between devices, body(): owned = lax.all_to_all(pieces, STRETCH, 0, 0, tiled=True)  6.02 us
    pallas_call x1, Pallas kernels, body(): kernel_call(reader_kernel, [SMEM] + [VMEM] * 5, [((HEADS // 2, KEYS, 2 *...  3.53 us
    pallas_call x1, Pallas kernels, body(): kernel_call(beacon_grad_kernel, [VMEM] * 4 + [HBM] + [VMEM] * 3, [((KEYS,...  2.98 us
  transfers between devices with their start and end apart: 26, of which 14 were waited for; matrix products, arithmetic and copies ran while one was open for 3% of the time, Pallas kernels for 20%

profile of v2, /device:TPU:0, one launch (start us, length us, event | category | flops | bytes accessed | tf_op | source)
XLA Modules:
  0.0 107.9 jit_solution(4231946839097920904)
XLA Ops:
  0.7 0.8 fusion
  1.5 0.8 broadcast_in_dim.2
  2.2 7.1 %all-to-all-start = ((bf16[16,48,256]{2,1,0:T(8,128)(2,1)}), bf16[16,48,256]{2,1,0:T(8,128)(2,1)S(1)}, u32[]{:S(2)}, u32[]{:S(2)}) async-start(bf16[16,48,256]{2,1,0:T(8,128)(2,1)} %broadcast_in_dim.2), calls=%async_computation | async-start | bytes 786432 | tf_op jit(solution)/shard_map/all_to_all | solution.py:322
  9.4 0.0 copy-start.5
  9.4 3.2 %collective-permute-start.3 = (bf16[256,512]{1,0:T(8,128)(2,1)S(1)}, bf16[256,512]{1,0:T(8,128)(2,1)S(1)}, u32[]{:S(2)}, u32[]{:S(2)}) collective-permute-start(bf16[256,512]{1,0:T(8,128)(2,1)S(1)} %convert_element_type.27.w_0), channel_id=1, source_target_pairs={{0,96},{32,0},{64,32},{96,64},{1,97},{33,1},{65,33},{97,65},{2,98}... | collective-permute-start | bytes 786440 | tf_op jit(solution)/shard_map/ppermute | solution.py:53
  12.6 0.9 collective-permute-start.2
  13.5 0.9 collective-permute-start.1
  14.4 0.1 stack.23.place
  14.4 0.6 shard_map.119
  15.0 0.1 collective-permute-start
  15.1 1.0 pad.7.q
  16.2 0.0 copy-start.2
  16.2 0.0 copy-start.3
  16.2 1.1 %pad.8.d = bf16[1792,128]{1,0:T(8,128)(2,1)S(1)} pad(bf16[1728,128]{1,0:T(8,128)(2,1)} %bitcast.37, bf16[]{:T(256)} %constant.20.clone.1), padding=0_64x0_0 | pad | bytes 901122 | tf_op jit(solution)/shard_map/jit(_pad)/pad | solution.py:337
  17.3 0.0 collective-permute-done.got
  17.3 5.6 %collective-permute-done.3.w_3 = bf16[256,512]{1,0:T(8,128)(2,1)S(1)} collective-permute-done((bf16[256,512]{1,0:T(8,128)(2,1)S(1)}, bf16[256,512]{1,0:T(8,128)(2,1)S(1)}, u32[]{:S(2)}, u32[]{:S(2)}) %collective-permute-start.3) | collective-permute-done | bytes 262176 | tf_op jit(solution)/shard_map/ppermute | solution.py:53
  22.9 1.5 %collective-permute-done.2.w_2 = bf16[256,512]{1,0:T(8,128)(2,1)S(1)} collective-permute-done((bf16[256,512]{1,0:T(8,128)(2,1)S(1)}, bf16[256,512]{1,0:T(8,128)(2,1)S(1)}, u32[]{:S(2)}, u32[]{:S(2)}) %collective-permute-start.2) | collective-permute-done | bytes 262176 | tf_op jit(solution)/shard_map/ppermute | solution.py:53
  24.4 3.9 %collective-permute-done.1.w_1 = bf16[256,512]{1,0:T(8,128)(2,1)S(1)} collective-permute-done((bf16[256,512]{1,0:T(8,128)(2,1)S(1)}, bf16[256,512]{1,0:T(8,128)(2,1)S(1)}, u32[]{:S(2)}, u32[]{:S(2)}) %collective-permute-start.1) | collective-permute-done | bytes 262176 | tf_op jit(solution)/shard_map/ppermute | solution.py:53
  28.3 3.5 %shard_map.120 = (f32[2,768,256]{2,1,0:T(8,128)S(1)}, bf16[128,768]{1,0:T(8,128)(2,1)S(1)}, bf16[128,768]{1,0:T(8,128)(2,1)S(1)}, bf16[128,768]{1,0:T(8,128)(2,1)S(1)}, bf16[128,768]{1,0:T(8,128)(2,1)S(1)}) custom-call(s32[5]{0:T(128)S(1)} %stack.23.place, s32[1,512]{1,0:T(1,128)S(1)} %bitcast.30, f32[512,128]{1,0:T(8,128)S(1)} %bitcast.28, ...), custom_call_target="tpu_custom_call" | custom-call | flops 503316480 | bytes 3145728 | tf_op jit(solution)/shard_map/pallas_call | solution.py:345
  31.8 1.5 %collective-permute-start.4 = (bf16[128,768]{1,0:T(8,128)(2,1)S(1)}, bf16[128,768]{1,0:T(8,128)(2,1)S(1)}, u32[]{:S(2)}, u32[]{:S(2)}) collective-permute-start(bf16[128,768]{1,0:T(8,128)(2,1)S(1)} %get-tuple-element.97), channel_id=1, source_target_pairs={{0,8},{8,16},{16,24},{24,0},{1,9},{9,17},{17,25},{25,1},{2,10},{10... | collective-permute-start | bytes 589832 | tf_op jit(solution)/shard_map/ppermute | solution.py:53
  33.4 2.7 %collective-permute-start.5 = (bf16[128,768]{1,0:T(8,128)(2,1)S(1)}, bf16[128,768]{1,0:T(8,128)(2,1)S(1)}, u32[]{:S(2)}, u32[]{:S(2)}) collective-permute-start(bf16[128,768]{1,0:T(8,128)(2,1)S(1)} %get-tuple-element.98), channel_id=1, source_target_pairs={{0,16},{8,24},{16,0},{24,8},{1,17},{9,25},{17,1},{25,9},{2,18},{10... | collective-permute-start | bytes 589832 | tf_op jit(solution)/shard_map/ppermute | solution.py:53
  36.0 1.5 %collective-permute-start.6 = (bf16[128,768]{1,0:T(8,128)(2,1)S(1)}, bf16[128,768]{1,0:T(8,128)(2,1)S(1)}, u32[]{:S(2)}, u32[]{:S(2)}) collective-permute-start(bf16[128,768]{1,0:T(8,128)(2,1)S(1)} %get-tuple-element.99), channel_id=1, source_target_pairs={{0,24},{8,0},{16,8},{24,16},{1,25},{9,1},{17,9},{25,17},{2,26},{10... | collective-permute-start | bytes 589832 | tf_op jit(solution)/shard_map/ppermute | solution.py:53
  37.5 3.5 %shard_map.121 = (f32[1728,128]{1,0:T(8,128)}, f32[768,256]{1,0:T(8,128)S(1)}, f32[432,256]{1,0:T(8,128)S(1)}) custom-call(s32[5]{0:T(128)S(1)} %stack.23.place, bf16[1792,128]{1,0:T(8,128)(2,1)S(1)} %pad.7.q, bf16[1792,128]{1,0:T(8,128)(2,1)S(1)} %pad.8.d, bf16[768,256]{1,0:T(8,128)(2,1)S(1)} %bitcast.22, bf16[432,256]{1,0:T(8,128)(2,1)S(1)} %pad_maximum_fusion.own_kv), custom_call_target="tpu_custom_call" | custom-call | flops 786432000 | bytes 4194304 | tf_op jit(solution)/shard_map/pallas_call | solution.py:359
  41.1 0.0 collective-permute-done.4.a_1
  41.1 3.6 %collective-permute-done.5.a_2 = bf16[128,768]{1,0:T(8,128)(2,1)S(1)} collective-permute-done((bf16[128,768]{1,0:T(8,128)(2,1)S(1)}, bf16[128,768]{1,0:T(8,128)(2,1)S(1)}, u32[]{:S(2)}, u32[]{:S(2)}) %collective-permute-start.5) | collective-permute-done | bytes 196640 | tf_op jit(solution)/shard_map/ppermute | solution.py:53
  44.7 0.0 collective-permute-done.6.a_3
  44.7 1.5 %shard_map.122 = (f32[512,128]{1,0:T(8,128)S(1)}, f32[512,128]{1,0:T(8,128)S(1)}, f32[512,128]{1,0:T(8,128)S(1)}, f32[512,128]{1,0:T(8,128)S(1)}, bf16[4,512,128...) custom-call(s32[5]{0:T(128)S(1)} %stack.23.place, ...), custom_call_target="tpu_custom_call" | custom-call | flops 536870912 | bytes 3145728 | tf_op jit(solution)/shard_map/pallas_call | solution.py:385
  46.3 0.1 collective-permute-start.7
  46.3 1.9 %collective-permute-done.7.other = bf16[4,512,128]{2,1,0:T(8,128)(2,1)S(1)} collective-permute-done((bf16[4,512,128]{2,1,0:T(8,128)(2,1)S(1)}, bf16[4,512,128]{2,1,0:T(8,128)(2,1)S(1)}, u32[]{:S(2)}, u32[]{:S(2)}) %collective-permute-start.7) | collective-permute-done | bytes 524320 | tf_op jit(solution)/shard_map/ppermute | solution.py:402
  48.2 0.1 shard_map.123
  48.3 2.0 %collective-permute-start.8 = (bf16[512,128]{1,0:T(8,128)(2,1)S(1)}, bf16[512,128]{1,0:T(8,128)(2,1)S(1)}, u32[]{:S(2)}, u32[]{:S(2)}) collective-permute-start(bf16[512,128]{1,0:T(8,128)(2,1)S(1)} %get-tuple-element.120), channel_id=1, source_target_pairs={{0,2},{2,4},{4,6},{6,0},{1,3},{3,5},{5,7},{7,1},{8,10},{10,12},{12... | collective-permute-start | bytes 393224 | tf_op jit(solution)/shard_map/ppermute | solution.py:53
  50.3 3.6 %collective-permute-start.9 = (bf16[512,128]{1,0:T(8,128)(2,1)S(1)}, bf16[512,128]{1,0:T(8,128)(2,1)S(1)}, u32[]{:S(2)}, u32[]{:S(2)}) collective-permute-start(bf16[512,128]{1,0:T(8,128)(2,1)S(1)} %get-tuple-element.121), channel_id=1, source_target_pairs={{0,4},{2,6},{4,0},{6,2},{1,5},{3,7},{5,1},{7,3},{8,12},{10,14},{12... | collective-permute-start | bytes 393224 | tf_op jit(solution)/shard_map/ppermute | solution.py:53
  53.9 1.0 collective-permute-start.10
  54.9 3.8 %shard_map.124 = (f32[1728,128]{1,0:T(8,128)}, f32[768,256]{1,0:T(8,128)S(1)}, f32[432,256]{1,0:T(8,128)S(1)}) custom-call(s32[5]{0:T(128)S(1)} %stack.23.place, bf16[1792,128]{1,0:T(8,128)(2,1)S(1)} %pad.7.q, bf16[1792,128]{1,0:T(8,128)(2,1)S(1)} %pad.8.d, ...), custom_call_target="tpu_custom_call", output_to_operand_aliasing={{0}: (5, {}), {1}: (6, {}), {2}: (7, {})} | custom-call | flops 786432000 | bytes 4194304 | tf_op jit(solution)/shard_map/pallas_call | solution.py:359
  58.7 1.5 %collective-permute-done.9 = bf16[512,128]{1,0:T(8,128)(2,1)S(1)} collective-permute-done((bf16[512,128]{1,0:T(8,128)(2,1)S(1)}, bf16[512,128]{1,0:T(8,128)(2,1)S(1)}, u32[]{:S(2)}, u32[]{:S(2)}) %collective-permute-start.9) | collective-permute-done | bytes 131104 | tf_op jit(solution)/shard_map/ppermute | solution.py:53
  60.2 0.1 add_convert_fusion.e_0
  60.3 2.4 %collective-permute-start.13 = (bf16[512,128]{1,0:T(8,128)(2,1)S(1)}, bf16[512,128]{1,0:T(8,128)(2,1)S(1)}, u32[]{:S(2)}, u32[]{:S(2)}) collective-permute-start(bf16[512,128]{1,0:T(8,128)(2,1)S(1)} %add_convert_fusion.e_0), channel_id=1, source_target_pairs={{0,6},{2,0},{4,2},{6,4},{1,7},{3,1},{5,3},{7,5},{8,14},{10,8},{12,... | collective-permute-start | bytes 393224 | tf_op jit(solution)/shard_map/ppermute | solution.py:53
  62.7 1.1 %collective-permute-start.12 = (bf16[512,128]{1,0:T(8,128)(2,1)S(1)}, bf16[512,128]{1,0:T(8,128)(2,1)S(1)}, u32[]{:S(2)}, u32[]{:S(2)}) collective-permute-start(bf16[512,128]{1,0:T(8,128)(2,1)S(1)} %add_convert_fusion.e_0), channel_id=1, source_target_pairs={{0,4},{2,6},{4,0},{6,2},{1,5},{3,7},{5,1},{7,3},{8,12},{10,14},{12... | collective-permute-start | bytes 393224 | tf_op jit(solution)/shard_map/ppermute | solution.py:53
  63.8 0.4 collective-permute-start.11
  64.2 3.5 %shard_map.125 = (f32[1728,128]{1,0:T(8,128)}, f32[768,256]{1,0:T(8,128)S(1)}, f32[432,256]{1,0:T(8,128)S(1)}) custom-call(s32[5]{0:T(128)S(1)} %stack.23.place, bf16[1792,128]{1,0:T(8,128)(2,1)S(1)} %pad.7.q, bf16[1792,128]{1,0:T(8,128)(2,1)S(1)} %pad.8.d, ...), custom_call_target="tpu_custom_call", output_to_operand_aliasing={{0}: (5, {}), {1}: (6, {}), {2}: (7, {})} | custom-call | flops 589824000 | bytes 4194304 | tf_op jit(solution)/shard_map/pallas_call | solution.py:359
  67.7 0.3 collective-permute-done.13.e_3
  68.1 2.3 %collective-permute-done.12.e_2 = bf16[512,128]{1,0:T(8,128)(2,1)S(1)} collective-permute-done((bf16[512,128]{1,0:T(8,128)(2,1)S(1)}, bf16[512,128]{1,0:T(8,128)(2,1)S(1)}, u32[]{:S(2)}, u32[]{:S(2)}) %collective-permute-start.12) | collective-permute-done | bytes 131104 | tf_op jit(solution)/shard_map/ppermute | solution.py:53
  70.4 1.4 %collective-permute-done.11.e_1 = bf16[512,128]{1,0:T(8,128)(2,1)S(1)} collective-permute-done((bf16[512,128]{1,0:T(8,128)(2,1)S(1)}, bf16[512,128]{1,0:T(8,128)(2,1)S(1)}, u32[]{:S(2)}, u32[]{:S(2)}) %collective-permute-start.11) | collective-permute-done | bytes 131104 | tf_op jit(solution)/shard_map/ppermute | solution.py:53
  71.7 0.5 collective-permute-start.16
  72.3 0.0 collective-permute-start.17
  72.3 0.8 collective-permute-done.15.o_1
  73.1 0.2 collective-permute-done.16.o_2
  73.3 0.3 collective-permute-done.17.o_3
  73.6 1.5 %shard_map.126 = (f32[128,512]{1,0:T(8,128)S(1)}, bf16[128,512]{1,0:T(8,128)(2,1)S(1)}, bf16[128,512]{1,0:T(8,128)(2,1)S(1)}, bf16[128,512]{1,0:T(8,128)(2,1)S(1)}) custom-call(s32[5]{0:T(128)S(1)} %stack.23.place, bf16[512,128]{1,0:T(8,128)(2,1)S(1)} %add_convert_fusion.e_0, bf16[512,128]{1,0:T(8,128)(2,1)S(1)} %collective-permute-done.11.e_1, ...), custom_call_target="tpu_custom_call" | custom-call | flops 536870912 | bytes 3145728 | tf_op jit(solution)/shard_map/pallas_call | solution.py:425
  75.1 2.5 %collective-permute-start.18 = (bf16[128,512]{1,0:T(8,128)(2,1)S(1)}, bf16[128,512]{1,0:T(8,128)(2,1)S(1)}, u32[]{:S(2)}, u32[]{:S(2)}) collective-permute-start(bf16[128,512]{1,0:T(8,128)(2,1)S(1)} %get-tuple-element.152), channel_id=1, source_target_pairs={{0,24},{8,0},{16,8},{24,16},{1,25},{9,1},{17,9},{25,17},{2,26},{10... | collective-permute-start | bytes 393224 | tf_op jit(solution)/shard_map/ppermute | solution.py:53
  77.6 1.1 %collective-permute-start.19 = (bf16[128,512]{1,0:T(8,128)(2,1)S(1)}, bf16[128,512]{1,0:T(8,128)(2,1)S(1)}, u32[]{:S(2)}, u32[]{:S(2)}) collective-permute-start(bf16[128,512]{1,0:T(8,128)(2,1)S(1)} %get-tuple-element.153), channel_id=1, source_target_pairs={{0,16},{8,24},{16,0},{24,8},{1,17},{9,25},{17,1},{25,9},{2,18},{10... | collective-permute-start | bytes 393224 | tf_op jit(solution)/shard_map/ppermute | solution.py:53
  78.8 0.5 collective-permute-start.20
  79.3 2.2 %shard_map.131 = (f32[256,512]{1,0:T(8,128)S(1)}, bf16[256,512]{1,0:T(8,128)(2,1)}, bf16[256,512]{1,0:T(8,128)(2,1)}, bf16[256,512]{1,0:T(8,128)(2,1)}) custom-call(s32[5]{0:T(128)S(1)} %stack.23.place, bf16[512,128]{1,0:T(8,128)(2,1)S(1)} %add_convert_fusion.e_0, bf16[512,128]{1,0:T(8,128)(2,1)S(1)} %collective-permute-done.11.e_1, ...), custom_call_target="tpu_custom_call" | custom-call | flops 536870912 | bytes 3145728 | tf_op jit(solution)/shard_map/pallas_call | solution.py:436
  81.6 0.1 collective-permute-start.21
  81.6 1.9 %collective-permute-start.22 = (bf16[256,512]{1,0:T(8,128)(2,1)}, bf16[256,512]{1,0:T(8,128)(2,1)S(1)}, u32[]{:S(2)}, u32[]{:S(2)}) collective-permute-start(bf16[256,512]{1,0:T(8,128)(2,1)} %get-tuple-element.165), channel_id=1, source_target_pairs={{0,64},{32,96},{64,0},{96,32},{1,65},{33,97},{65,1},{97,33},{2,66}... | collective-permute-start | bytes 786440 | tf_op jit(solution)/shard_map/ppermute | solution.py:53
  83.5 0.1 collective-permute-done.18.g_1
  83.6 1.7 %collective-permute-start.23 = (bf16[256,512]{1,0:T(8,128)(2,1)}, bf16[256,512]{1,0:T(8,128)(2,1)S(1)}, u32[]{:S(2)}, u32[]{:S(2)}) collective-permute-start(bf16[256,512]{1,0:T(8,128)(2,1)} %get-tuple-element.166), channel_id=1, source_target_pairs={{0,96},{32,0},{64,32},{96,64},{1,97},{33,1},{65,33},{97,65},{2,98}... | collective-permute-start | bytes 786440 | tf_op jit(solution)/shard_map/ppermute | solution.py:53
  85.3 3.6 %shard_map.127 = (f32[1728,128]{1,0:T(8,128)}, f32[768,256]{1,0:T(8,128)S(1)}, f32[432,256]{1,0:T(8,128)S(1)}) custom-call(s32[5]{0:T(128)S(1)} %stack.23.place, bf16[1792,128]{1,0:T(8,128)(2,1)S(1)} %pad.7.q, bf16[1792,128]{1,0:T(8,128)(2,1)S(1)} %pad.8.d, ...), custom_call_target="tpu_custom_call", output_to_operand_aliasing={{0}: (5, {}), {1}: (6, {}), {2}: (7, {})} | custom-call | flops 589824000 | bytes 4194304 | tf_op jit(solution)/shard_map/pallas_call | solution.py:359
  88.9 3.0 %shard_map.128 = (bf16[768,512]{1,0:T(8,128)(2,1)S(1)}, bf16[768,256]{1,0:T(8,128)(2,1)}) custom-call(f32[128,512]{1,0:T(8,128)S(1)} %get-tuple-element.151.g_0, bf16[128,512]{1,0:T(8,128)(2,1)S(1)} %collective-permute-done.18.g_1, bf16[128,512]{1,0:T(8,128)(2,1)S(1)} %collective-permute-done.19.g_2, bf16[128,512]{1,0:T(8,128)(2,1)S(1)} %collective-permute-done.20.g_3, ...), custom_call_target="tpu_custom_call" | custom-call | flops 402653184 | bytes 5242880 | tf_op jit(solution)/shard_map/pallas_call | solution.py:450
  91.9 6.0 %all-to-all-start.1 = ((bf16[16,48,256]{2,1,0:T(8,128)(2,1)}), bf16[16,48,256]{2,1,0:T(8,128)(2,1)S(1)}, u32[]{:S(2)}, u32[]{:S(2)}) async-start(bf16[16,48,256]{2,1,0:T(8,128)(2,1)} %bitcast.14), calls=%async_computation.1 | async-start | bytes 786432 | tf_op jit(solution)/shard_map/all_to_all | solution.py:460
  98.0 1.2 %shard_map.130 = f32[128,4,128]{2,1,0:T(4,128)} custom-call(bf16[768,512]{1,0:T(8,128)(2,1)S(1)} %get-tuple-element.160.score_grad, bf16[768,256]{1,0:T(8,128)(2,1)S(1)} %bitcast.27), custom_call_target="tpu_custom_call" | custom-call | flops 100663296 | bytes 2097152 | tf_op jit(solution)/shard_map/pallas_call | solution.py:461
  99.2 0.9 convert_add_fusion
  100.1 7.0 %all-to-all-done.1.owned = bf16[16,48,256]{2,1,0:T(8,128)(2,1)S(1)} async-done(((bf16[16,48,256]{2,1,0:T(8,128)(2,1)}), bf16[16,48,256]{2,1,0:T(8,128)(2,1)S(1)}, u32[]{:S(2)}, u32[]{:S(2)}) %all-to-all-start.1) | async-done | bytes 393248 | tf_op jit(solution)/shard_map/all_to_all | solution.py:460
  107.1 0.8 shard_map.129
  (25 shorter events, 0.1 us)
Async XLA Ops:
  0.6 8.7 %copy-start.1 = (f32[256,512]{1,0:T(8,128)S(1)}, f32[256,512]{1,0:T(8,128)}, u32[]{:S(2)}) copy-start(f32[256,512]{1,0:T(8,128)} %param.15) | copy-start | bytes 1572868
  0.6 13.8 %copy-start = (f32[128,512]{1,0:T(8,128)S(1)}, f32[128,512]{1,0:T(8,128)}, u32[]{:S(2)}) copy-start(f32[128,512]{1,0:T(8,128)} %target.1) | copy-start | bytes 786436
  0.7 14.5 %copy-start.4 = (f32[128,4,128]{2,1,0:T(4,128)S(1)}, f32[128,4,128]{2,1,0:T(4,128)}, u32[]{:S(2)}) copy-start(f32[128,4,128]{2,1,0:T(4,128)} %param.12) | copy-start | bytes 786436
  2.2 26.0 %all-to-all-start = ((bf16[16,48,256]{2,1,0:T(8,128)(2,1)}), bf16[16,48,256]{2,1,0:T(8,128)(2,1)S(1)}, u32[]{:S(2)}, u32[]{:S(2)}) async-start(bf16[16,48,256]{2,1,0:T(8,128)(2,1)} %broadcast_in_dim.2), calls=%async_computation | async-start | bytes 786432 | tf_op jit(solution)/shard_map/all_to_all | solution.py:322
  9.4 7.9 %copy-start.5 = (s32[128]{0:T(128)S(1)}, s32[128]{0:T(128)}, u32[]{:S(2)}) copy-start(s32[128]{0:T(128)} %param.13) | copy-start | bytes 1540
  9.4 13.5 %collective-permute-start.3 = (bf16[256,512]{1,0:T(8,128)(2,1)S(1)}, bf16[256,512]{1,0:T(8,128)(2,1)S(1)}, u32[]{:S(2)}, u32[]{:S(2)}) collective-permute-start(bf16[256,512]{1,0:T(8,128)(2,1)S(1)} %convert_element_type.27.w_0), channel_id=1, source_target_pairs={{0,96},{32,0},{64,32},{96,64},{1,97},{33,1},{65,33},{97,65},{2,98}... | collective-permute-start | bytes 786440 | tf_op jit(solution)/shard_map/ppermute | solution.py:53
  12.6 11.8 %collective-permute-start.2 = (bf16[256,512]{1,0:T(8,128)(2,1)S(1)}, bf16[256,512]{1,0:T(8,128)(2,1)S(1)}, u32[]{:S(2)}, u32[]{:S(2)}) collective-permute-start(bf16[256,512]{1,0:T(8,128)(2,1)S(1)} %convert_element_type.27.w_0), channel_id=1, source_target_pairs={{0,64},{32,96},{64,0},{96,32},{1,65},{33,97},{65,1},{97,33},{2,66}... | collective-permute-start | bytes 786440 | tf_op jit(solution)/shard_map/ppermute | solution.py:53
  13.5 14.8 %collective-permute-start.1 = (bf16[256,512]{1,0:T(8,128)(2,1)S(1)}, bf16[256,512]{1,0:T(8,128)(2,1)S(1)}, u32[]{:S(2)}, u32[]{:S(2)}) collective-permute-start(bf16[256,512]{1,0:T(8,128)(2,1)S(1)} %convert_element_type.27.w_0), channel_id=1, source_target_pairs={{0,32},{32,64},{64,96},{96,0},{1,33},{33,65},{65,97},{97,1},{2,34}... | collective-permute-start | bytes 786440 | tf_op jit(solution)/shard_map/ppermute | solution.py:53
  15.0 2.3 %collective-permute-start = (f32[2,128,128]{2,1,0:T(8,128)S(1)}, f32[2,128,128]{2,1,0:T(8,128)S(1)}, u32[]{:S(2)}, u32[]{:S(2)}) collective-permute-start(f32[2,128,128]{2,1,0:T(8,128)S(1)} %get-tuple-element.87), channel_id=1, source_target_pairs={{0,1},{1,0},{2,3},{3,2},{4,5},{5,4},{6,7},{7,6},{8,9},{9,8},{10,11... | collective-permute-start | bytes 393224 | tf_op jit(solution)/shard_map/ppermute | solution.py:333
  16.2 21.3 %copy-start.2 = (bf16[1,432,1,128]{3,1,2,0:T(8,128)(2,1)S(1)}, bf16[1,432,1,128]{3,1,2,0:T(8,128)(2,1)}, u32[]{:S(2)}) copy-start(bf16[1,432,1,128]{3,1,2,0:T(8,128)(2,1)} %param.9) | copy-start | bytes 331780
  16.2 21.3 %copy-start.3 = (bf16[1,432,1,128]{3,1,2,0:T(8,128)(2,1)S(1)}, bf16[1,432,1,128]{3,1,2,0:T(8,128)(2,1)}, u32[]{:S(2)}) copy-start(bf16[1,432,1,128]{3,1,2,0:T(8,128)(2,1)} %param.10) | copy-start | bytes 331780
  31.8 9.3 %collective-permute-start.4 = (bf16[128,768]{1,0:T(8,128)(2,1)S(1)}, bf16[128,768]{1,0:T(8,128)(2,1)S(1)}, u32[]{:S(2)}, u32[]{:S(2)}) collective-permute-start(bf16[128,768]{1,0:T(8,128)(2,1)S(1)} %get-tuple-element.97), channel_id=1, source_target_pairs={{0,8},{8,16},{16,24},{24,0},{1,9},{9,17},{17,25},{25,1},{2,10},{10... | collective-permute-start | bytes 589832 | tf_op jit(solution)/shard_map/ppermute | solution.py:53
  33.4 11.3 %collective-permute-start.5 = (bf16[128,768]{1,0:T(8,128)(2,1)S(1)}, bf16[128,768]{1,0:T(8,128)(2,1)S(1)}, u32[]{:S(2)}, u32[]{:S(2)}) collective-permute-start(bf16[128,768]{1,0:T(8,128)(2,1)S(1)} %get-tuple-element.98), channel_id=1, source_target_pairs={{0,16},{8,24},{16,0},{24,8},{1,17},{9,25},{17,1},{25,9},{2,18},{10... | collective-permute-start | bytes 589832 | tf_op jit(solution)/shard_map/ppermute | solution.py:53
  36.0 8.7 %collective-permute-start.6 = (bf16[128,768]{1,0:T(8,128)(2,1)S(1)}, bf16[128,768]{1,0:T(8,128)(2,1)S(1)}, u32[]{:S(2)}, u32[]{:S(2)}) collective-permute-start(bf16[128,768]{1,0:T(8,128)(2,1)S(1)} %get-tuple-element.99), channel_id=1, source_target_pairs={{0,24},{8,0},{16,8},{24,16},{1,25},{9,1},{17,9},{25,17},{2,26},{10... | collective-permute-start | bytes 589832 | tf_op jit(solution)/shard_map/ppermute | solution.py:53
  46.3 2.0 %collective-permute-start.7 = (bf16[4,512,128]{2,1,0:T(8,128)(2,1)S(1)}, bf16[4,512,128]{2,1,0:T(8,128)(2,1)S(1)}, u32[]{:S(2)}, u32[]{:S(2)}) collective-permute-start(bf16[4,512,128]{2,1,0:T(8,128)(2,1)S(1)} %get-tuple-element.116), channel_id=1, source_target_pairs={{0,1},{1,0},{2,3},{3,2},{4,5},{5,4},{6,7},{7,6},{8,9},{9,8},{10,11... | collective-permute-start | bytes 1572872 | tf_op jit(solution)/shard_map/ppermute | solution.py:402
  48.3 10.3 %collective-permute-start.8 = (bf16[512,128]{1,0:T(8,128)(2,1)S(1)}, bf16[512,128]{1,0:T(8,128)(2,1)S(1)}, u32[]{:S(2)}, u32[]{:S(2)}) collective-permute-start(bf16[512,128]{1,0:T(8,128)(2,1)S(1)} %get-tuple-element.120), channel_id=1, source_target_pairs={{0,2},{2,4},{4,6},{6,0},{1,3},{3,5},{5,7},{7,1},{8,10},{10,12},{12... | collective-permute-start | bytes 393224 | tf_op jit(solution)/shard_map/ppermute | solution.py:53
  50.3 9.9 %collective-permute-start.9 = (bf16[512,128]{1,0:T(8,128)(2,1)S(1)}, bf16[512,128]{1,0:T(8,128)(2,1)S(1)}, u32[]{:S(2)}, u32[]{:S(2)}) collective-permute-start(bf16[512,128]{1,0:T(8,128)(2,1)S(1)} %get-tuple-element.121), channel_id=1, source_target_pairs={{0,4},{2,6},{4,0},{6,2},{1,5},{3,7},{5,1},{7,3},{8,12},{10,14},{12... | collective-permute-start | bytes 393224 | tf_op jit(solution)/shard_map/ppermute | solution.py:53
  53.9 6.3 %collective-permute-start.10 = (bf16[512,128]{1,0:T(8,128)(2,1)S(1)}, bf16[512,128]{1,0:T(8,128)(2,1)S(1)}, u32[]{:S(2)}, u32[]{:S(2)}) collective-permute-start(bf16[512,128]{1,0:T(8,128)(2,1)S(1)} %get-tuple-element.122), channel_id=1, source_target_pairs={{0,6},{2,0},{4,2},{6,4},{1,7},{3,1},{5,3},{7,5},{8,14},{10,8},{12,... | collective-permute-start | bytes 393224 | tf_op jit(solution)/shard_map/ppermute | solution.py:53
  60.3 7.8 %collective-permute-start.13 = (bf16[512,128]{1,0:T(8,128)(2,1)S(1)}, bf16[512,128]{1,0:T(8,128)(2,1)S(1)}, u32[]{:S(2)}, u32[]{:S(2)}) collective-permute-start(bf16[512,128]{1,0:T(8,128)(2,1)S(1)} %add_convert_fusion.e_0), channel_id=1, source_target_pairs={{0,6},{2,0},{4,2},{6,4},{1,7},{3,1},{5,3},{7,5},{8,14},{10,8},{12,... | collective-permute-start | bytes 393224 | tf_op jit(solution)/shard_map/ppermute | solution.py:53
  62.7 7.7 %collective-permute-start.12 = (bf16[512,128]{1,0:T(8,128)(2,1)S(1)}, bf16[512,128]{1,0:T(8,128)(2,1)S(1)}, u32[]{:S(2)}, u32[]{:S(2)}) collective-permute-start(bf16[512,128]{1,0:T(8,128)(2,1)S(1)} %add_convert_fusion.e_0), channel_id=1, source_target_pairs={{0,4},{2,6},{4,0},{6,2},{1,5},{3,7},{5,1},{7,3},{8,12},{10,14},{12... | collective-permute-start | bytes 393224 | tf_op jit(solution)/shard_map/ppermute | solution.py:53
  63.8 7.9 %collective-permute-start.11 = (bf16[512,128]{1,0:T(8,128)(2,1)S(1)}, bf16[512,128]{1,0:T(8,128)(2,1)S(1)}, u32[]{:S(2)}, u32[]{:S(2)}) collective-permute-start(bf16[512,128]{1,0:T(8,128)(2,1)S(1)} %add_convert_fusion.e_0), channel_id=1, source_target_pairs={{0,2},{2,4},{4,6},{6,0},{1,3},{3,5},{5,7},{7,1},{8,10},{10,12},{12... | collective-permute-start | bytes 393224 | tf_op jit(solution)/shard_map/ppermute | solution.py:53
  64.2 8.1 %collective-permute-start.14 = (bf16[512,128]{1,0:T(8,128)(2,1)S(1)}, bf16[512,128]{1,0:T(8,128)(2,1)S(1)}, u32[]{:S(2)}, u32[]{:S(2)}) collective-permute-start(bf16[512,128]{1,0:T(8,128)(2,1)S(1)} %add_convert_fusion.e_0), channel_id=1, source_target_pairs={{0,1},{1,0},{2,3},{3,2},{4,5},{5,4},{6,7},{7,6},{8,9},{9,8},{10,11... | collective-permute-start | bytes 393224 | tf_op jit(solution)/shard_map/ppermute | solution.py:422
  71.7 1.3 %collective-permute-start.15 = (bf16[512,128]{1,0:T(8,128)(2,1)S(1)}, bf16[512,128]{1,0:T(8,128)(2,1)S(1)}, u32[]{:S(2)}, u32[]{:S(2)}) collective-permute-start(bf16[512,128]{1,0:T(8,128)(2,1)S(1)} %collective-permute-done.11.e_1), channel_id=1, source_target_pairs={{0,1},{1,0},{2,3},{3,2},{4,5},{5,4},{6,7},{7,6},{8,9},{9,8},{10,11... | collective-permute-start | bytes 393224 | tf_op jit(solution)/shard_map/ppermute | solution.py:422
  71.7 1.5 %collective-permute-start.16 = (bf16[512,128]{1,0:T(8,128)(2,1)S(1)}, bf16[512,128]{1,0:T(8,128)(2,1)S(1)}, u32[]{:S(2)}, u32[]{:S(2)}) collective-permute-start(bf16[512,128]{1,0:T(8,128)(2,1)S(1)} %collective-permute-done.12.e_2), channel_id=1, source_target_pairs={{0,1},{1,0},{2,3},{3,2},{4,5},{5,4},{6,7},{7,6},{8,9},{9,8},{10,11... | collective-permute-start | bytes 393224 | tf_op jit(solution)/shard_map/ppermute | solution.py:422
  72.3 1.3 %collective-permute-start.17 = (bf16[512,128]{1,0:T(8,128)(2,1)S(1)}, bf16[512,128]{1,0:T(8,128)(2,1)S(1)}, u32[]{:S(2)}, u32[]{:S(2)}) collective-permute-start(bf16[512,128]{1,0:T(8,128)(2,1)S(1)} %collective-permute-done.13.e_3), channel_id=1, source_target_pairs={{0,1},{1,0},{2,3},{3,2},{4,5},{5,4},{6,7},{7,6},{8,9},{9,8},{10,11... | collective-permute-start | bytes 393224 | tf_op jit(solution)/shard_map/ppermute | solution.py:422
  75.1 8.5 %collective-permute-start.18 = (bf16[128,512]{1,0:T(8,128)(2,1)S(1)}, bf16[128,512]{1,0:T(8,128)(2,1)S(1)}, u32[]{:S(2)}, u32[]{:S(2)}) collective-permute-start(bf16[128,512]{1,0:T(8,128)(2,1)S(1)} %get-tuple-element.152), channel_id=1, source_target_pairs={{0,24},{8,0},{16,8},{24,16},{1,25},{9,1},{17,9},{25,17},{2,26},{10... | collective-permute-start | bytes 393224 | tf_op jit(solution)/shard_map/ppermute | solution.py:53
  77.6 11.3 %collective-permute-start.19 = (bf16[128,512]{1,0:T(8,128)(2,1)S(1)}, bf16[128,512]{1,0:T(8,128)(2,1)S(1)}, u32[]{:S(2)}, u32[]{:S(2)}) collective-permute-start(bf16[128,512]{1,0:T(8,128)(2,1)S(1)} %get-tuple-element.153), channel_id=1, source_target_pairs={{0,16},{8,24},{16,0},{24,8},{1,17},{9,25},{17,1},{25,9},{2,18},{10... | collective-permute-start | bytes 393224 | tf_op jit(solution)/shard_map/ppermute | solution.py:53
  78.8 10.2 %collective-permute-start.20 = (bf16[128,512]{1,0:T(8,128)(2,1)S(1)}, bf16[128,512]{1,0:T(8,128)(2,1)S(1)}, u32[]{:S(2)}, u32[]{:S(2)}) collective-permute-start(bf16[128,512]{1,0:T(8,128)(2,1)S(1)} %get-tuple-element.154), channel_id=1, source_target_pairs={{0,8},{8,16},{16,24},{24,0},{1,9},{9,17},{17,25},{25,1},{2,10},{10... | collective-permute-start | bytes 393224 | tf_op jit(solution)/shard_map/ppermute | solution.py:53
  81.6 17.6 %collective-permute-start.21 = (bf16[256,512]{1,0:T(8,128)(2,1)}, bf16[256,512]{1,0:T(8,128)(2,1)S(1)}, u32[]{:S(2)}, u32[]{:S(2)}) collective-permute-start(bf16[256,512]{1,0:T(8,128)(2,1)} %get-tuple-element.164), channel_id=1, source_target_pairs={{0,32},{32,64},{64,96},{96,0},{1,33},{33,65},{65,97},{97,1},{2,34}... | collective-permute-start | bytes 786440 | tf_op jit(solution)/shard_map/ppermute | solution.py:53
  81.6 17.5 %collective-permute-start.22 = (bf16[256,512]{1,0:T(8,128)(2,1)}, bf16[256,512]{1,0:T(8,128)(2,1)S(1)}, u32[]{:S(2)}, u32[]{:S(2)}) collective-permute-start(bf16[256,512]{1,0:T(8,128)(2,1)} %get-tuple-element.165), channel_id=1, source_target_pairs={{0,64},{32,96},{64,0},{96,32},{1,65},{33,97},{65,1},{97,33},{2,66}... | collective-permute-start | bytes 786440 | tf_op jit(solution)/shard_map/ppermute | solution.py:53
  83.6 15.6 %collective-permute-start.23 = (bf16[256,512]{1,0:T(8,128)(2,1)}, bf16[256,512]{1,0:T(8,128)(2,1)S(1)}, u32[]{:S(2)}, u32[]{:S(2)}) collective-permute-start(bf16[256,512]{1,0:T(8,128)(2,1)} %get-tuple-element.166), channel_id=1, source_target_pairs={{0,96},{32,0},{64,32},{96,64},{1,97},{33,1},{65,33},{97,65},{2,98}... | collective-permute-start | bytes 786440 | tf_op jit(solution)/shard_map/ppermute | solution.py:53
  91.9 15.2 %all-to-all-start.1 = ((bf16[16,48,256]{2,1,0:T(8,128)(2,1)}), bf16[16,48,256]{2,1,0:T(8,128)(2,1)S(1)}, u32[]{:S(2)}, u32[]{:S(2)}) async-start(bf16[16,48,256]{2,1,0:T(8,128)(2,1)} %bitcast.14), calls=%async_computation.1 | async-start | bytes 786432 | tf_op jit(solution)/shard_map/all_to_all | solution.py:460
